TPU v7x, 128 devices: a whole 4x4x4 slice. The times are simulated.
128 devices in a mesh: dp: 16 (over x, z), ctx: 8 (over y, core).
Axes of the slice: x: 4, y: 4, z: 4, core: 2. Of those that a mesh axis runs over, the one named last changes fastest.
Arguments:
- patches: bfloat16 [4096, 5120], P('dp'), may hold values from -6 to 6
- vit_gain: float32 [1280], replicated, may hold values from 0.1 to 1.9
- merge_up: bfloat16 [5120, 3072], P(None, 'ctx'), may hold values from -0.078125 to 0.078125
- merge_down: bfloat16 [3072, 8192], P('ctx'), may hold values from -0.109375 to 0.109375
- dest: int32 [4096], P(('dp', 'ctx')), may hold values from 0 to 16383, as said below
- text: bfloat16 [16, 1024, 8192], P('dp', 'ctx'), may hold values from -6 to 6
- norm_gain: float32 [8192], replicated, may hold values from 0.5 to 1.5
- kv_weight: bfloat16 [8192, 1024], P(('dp', 'ctx')), may hold values from -0.0625 to 0.0625
- queries: bfloat16 [16, 1024, 4096], P('dp', 'ctx'), may hold values from -256 to 256
- out_grad: bfloat16 [16, 1024, 4096], P('dp', 'ctx'), may hold values from -6 to 6
- assign: int32 [16], replicated, may hold values from 0 to 15, each once
- docs: int32 [16, 1024], P('dp'), may hold values from 0 to 3, never falling along the last dimension, each value on 1 to 512 neighbouring positions
Outputs:
- attn_out: bfloat16 [16, 1024, 4096], P('dp', 'ctx')
- q_grad: bfloat16 [16, 1024, 4096], P('dp', 'ctx')
- hidden_grad: bfloat16 [16, 1024, 8192], P('dp', 'ctx')
- visual_grad: bfloat16 [4096, 8192], P(('dp', 'ctx'))
Inputs may be any that keep to these rules, and one draw needn't show every extreme that they name: `dest`: all entries are distinct. The 32 entries held by one device name rows of 32 devices' blocks of 128 rows per device (row // 128 names the device), each such device named by exactly one entry of the holding device. Every device's block receives exactly 32 entries, which fill one run of consecutive rows, in the order of the entries' index within their holding device.
All inputs are finite; a program needn't handle non-finite values.
Results may differ from a plain program's by a relative error of at most 0.035.
Values may be sent and summed in bfloat16 or wider, within the bound.
A program may use at most 192 MiB of HBM per device.

v0:
```python
import functools
import math

import jax
import jax.numpy as jnp
from jax import lax
from jax.experimental import pallas as pl
from jax.experimental.pallas import tpu as pltpu
from jax.sharding import PartitionSpec as P

MESH = pl.DeviceIdType.MESH
BF = jnp.bfloat16
F32 = jnp.float32
HEADS = 32
KVH = 4
HD = 128
GROUP = HEADS // KVH
EPS = 1e-06
ANY = pl.BlockSpec(memory_space=pl.ANY)
VM = pl.BlockSpec(memory_space=pltpu.VMEM)


def place():
    dp, ctx = lax.axis_index("dp"), lax.axis_index("ctx")
    return {"x": dp // 4, "z": dp % 4, "y": ctx // 2, "k": ctx % 2}


def device(at):
    return (at["x"] * 4 + at["z"], at["y"] * 2 + at["k"])


def shifted(at, axis, by):
    size = 2 if axis == "k" else 4
    return dict(at, **{axis: lax.rem(at[axis] + by + size, size)})


def remote(src, dst, send, recv, to):
    return pltpu.make_async_remote_copy(
        src_ref=src, dst_ref=dst, send_sem=send, recv_sem=recv, device_id=to, device_id_type=MESH
    )


def greet(devices):
    barrier = pltpu.get_barrier_semaphore()
    for to in devices:
        pl.semaphore_signal(barrier, inc=1, device_id=to, device_id_type=MESH)
    pl.semaphore_wait(barrier, len(devices))


class Ring:
    def __init__(self, at, axis, slab, send, recv, base):
        self.at, self.axis, self.slab, self.send, self.recv, self.base = at, axis, slab, send, recv, base
        self.plus, self.minus = device(shifted(at, axis, 1)), device(shifted(at, axis, -1))
        self.sent = []

    def _coordinate(self, by):
        return shifted(self.at, self.axis, by)[self.axis]

    def _copy(self, by, half, number, to):
        ref = self.slab(self._coordinate(by), half)
        copy = remote(ref, ref, self.send.at[self.base + number], self.recv.at[self.base + number], to)
        copy.start()
        self.sent.append(copy)

    def start(self):
        self._copy(0, 0, 0, self.plus)
        self._copy(0, 1, 1, self.minus)
        self._copy(0, 1, 2, self.plus)
        self._copy(0, 0, 3, self.minus)

    ARRIVALS = ((-1, 0), (1, 1), (-1, 1), (1, 0), (2, 0), (2, 1))

    def arrived(self, number):
        by, half = self.ARRIVALS[number]
        ref = self.slab(self._coordinate(by), half)
        remote(ref, ref, self.send.at[self.base + number], self.recv.at[self.base + number], self.plus).wait_recv()
        return ref

    def relay(self):
        first, second = self.arrived(0), self.arrived(1)
        self._copy(-1, 0, 4, self.plus)
        self._copy(1, 1, 5, self.minus)
        return first, second

    def finish(self):
        for copy in self.sent:
            copy.wait_send()


class RingSum:
    def __init__(self, at, sums, far, plain, through, chunks, send, recv):
        self.at, self.sums, self.far, self.plain, self.through = at, sums, far, plain, through
        self.chunks, self.send, self.recv = chunks, send, recv
        self.width = sums.shape[2] // chunks
        self.sent = []

    def _block(self, by, chunk):
        y = shifted(self.at, "y", by)["y"]
        return self.sums.at[y, :, pl.ds(chunk * self.width, self.width)]

    def _way(self, chunk):
        return 1 if chunk < self.chunks // 2 else -1

    def _copy(self, src, dst, number, by):
        copy = remote(src, dst, self.send.at[number], self.recv.at[number], device(shifted(self.at, "y", by)))
        copy.start()
        self.sent.append(copy)

    def _wait(self, dst, number):
        remote(dst, dst, self.send.at[number], self.recv.at[number], device(shifted(self.at, "y", 1))).wait_recv()

    def start(self, chunk):
        way = self._way(chunk)
        self._copy(self._block(2, chunk), self.far.at[chunk], chunk * 3, way)
        self._copy(self._block(-way, chunk), self.plain.at[chunk], chunk * 3 + 1, -way)

    def relay(self, chunk):
        way = self._way(chunk)
        self._wait(self.far.at[chunk], chunk * 3)
        block = self._block(way, chunk)
        block[...] = (block[...].astype(F32) + self.far[chunk].astype(F32)).astype(BF)
        self._copy(block, self.through.at[chunk], chunk * 3 + 2, way)

    def total(self, chunk):
        self._wait(self.plain.at[chunk], chunk * 3 + 1)
        self._wait(self.through.at[chunk], chunk * 3 + 2)
        own = self._block(0, chunk)[...].astype(F32)
        return own + self.plain[chunk].astype(F32) + self.through[chunk].astype(F32)

    def finish(self):
        for copy in self.sent:
            copy.wait_send()


PARTS = ((0, 384, "yzx"), (384, 384, "yxz"), (768, 256, "xzy"))
ORDER = (0, 2, 1, 3)


def first_kernel(
    patches_hbm, vit_gain, up_hbm, down_hbm, text_hbm, gain, kv_hbm, slot_of, row_of,
    weight_out, outgoing, text_pairs, visual_pairs, visual_out, scales,
    weight, patches, up, down, text, normed, hidden, partial, from_partner, sums, far, plain, through, acc, inner,
    load, send, recv, forward_send, forward_recv, pair_send, pair_recv, sum_send, sum_recv,
):
    at = place()
    k, y = at["k"], at["y"]
    chip = (at["x"] * 4 + at["z"]) * 4 + y
    own = pltpu.make_async_copy(kv_hbm, weight.at[chip, k], load.at[0])
    own.start()
    loads = []
    for number, (src, dst) in enumerate(((patches_hbm, patches), (up_hbm, up), (down_hbm, down), (text_hbm, text))):
        copy = pltpu.make_async_copy(src, dst, load.at[number + 1])
        copy.start()
        loads.append(copy)
    partner = device(shifted(at, "k", 1))
    greet([device(shifted(at, axis, by)) for axis in "xyz" for by in (1, -1)] + [partner])
    own.wait()

    def slab_of(axes_done, axis, first, count):
        def slab(coordinate, half):
            cut = {name: (pl.ds(0, 4) if name in axes_done else pl.ds(at[name], 1)) for name in "xyz"}
            cut[axis] = pl.ds(coordinate, 1)
            view = weight.reshape(4, 4, 4, 2, 64, 1024) if False else weight6
            return view.at[cut["x"], cut["z"], cut["y"], k, pl.ds(32 * half, 32), pl.ds(first, count)]

        return slab

    weight6 = weight.reshape(4, 4, 4, 2, 64, 1024)
    rings = [
        [
            Ring(at, order[phase], slab_of(order[:phase], order[phase], first, count), send, recv, (part * 3 + phase) * 6)
            for phase in range(3)
        ]
        for part, (first, count, order) in enumerate(PARTS)
    ]
    forwards = []

    def forward(ref, number):
        copy = remote(ref, ref, forward_send.at[number], forward_recv.at[number], partner)
        copy.start()
        forwards.append(copy)

    for part in rings:
        part[0].start()

    loads[0].wait()
    vg = vit_gain[...]

    def norm_rows(step, carry):
        rows = pl.ds(pl.multiple_of(step * 16, 16), 16)
        for piece in range(4):
            columns = pl.ds(piece * 1280, 1280)
            value = patches[rows, columns].astype(F32)
            center = value - jnp.mean(value, axis=-1, keepdims=True)
            spread = jnp.mean(center * center, axis=-1, keepdims=True)
            patches[rows, columns] = (center * lax.rsqrt(spread + EPS) * vg).astype(BF)
        return carry

    lax.fori_loop(0, 16, norm_rows, 0)
    for part in rings:
        part[0].relay()

    loads[1].wait()
    inner[...] = jnp.zeros_like(inner)

    def up_step(step, carry):
        columns = pl.ds(pl.multiple_of(step * 1024, 1024), 1024)
        inner[...] += jnp.dot(patches[:, columns], up[columns, :], preferred_element_type=F32)
        return carry

    lax.fori_loop(0, 5, up_step, 0)
    for part in rings:
        for number in (2, 3, 4, 5):
            part[0].arrived(number)
        part[1].start()
    value = inner[...]
    hidden[...] = (0.5 * value * (1.0 + lax.erf(value * (1.0 / math.sqrt(2.0))))).astype(BF)
    loads[2].wait()

    width = 2048
    swaps = {}
    for chunk in ORDER:
        def down_step(step, carry, chunk=chunk):
            columns = pl.ds(pl.multiple_of(chunk * width + step * 512, 512), 512)
            product = jnp.dot(hidden[...], down[:, columns], preferred_element_type=F32)
            partial[:, :, :, columns] = product.astype(BF).reshape(4, 2, 32, 512)
            return carry

        lax.fori_loop(0, 4, down_step, 0)
        columns = pl.ds(chunk * width, width)
        swaps[chunk] = remote(
            partial.at[:, 1 - k, :, columns], from_partner.at[:, :, columns], pair_send.at[chunk], pair_recv.at[chunk], partner
        )
        swaps[chunk].start()
        if chunk == 2:
            for part in rings:
                part[1].relay()
    ring_sum = RingSum(at, sums, far, plain, through, 4, sum_send, sum_recv)
    for chunk in ORDER:
        swaps[chunk].wait_recv()
        columns = pl.ds(chunk * width, width)
        for block in range(4):
            mine = partial[block, pl.ds(k, 1), :, columns].reshape(32, width)
            sums[block, :, columns] = (mine.astype(F32) + from_partner[block, :, columns].astype(F32)).astype(BF)
        ring_sum.start(chunk)
    for number, part in enumerate(rings):
        for arrival in (2, 3, 4, 5):
            part[1].arrived(arrival)
        part[2].start()
        order = PARTS[number][2]
        cut = {name: (pl.ds(at[name], 1) if name == order[2] else pl.ds(0, 4)) for name in "xyz"}
        forward(weight6.at[cut["x"], cut["z"], cut["y"], k, :, pl.ds(PARTS[number][0], PARTS[number][1])], number * 7)

    loads[3].wait()

    def text_rows(step, carry):
        rows = pl.ds(pl.multiple_of(step * 16, 16), 16)
        value = text[rows, :].astype(F32)
        scale = lax.rsqrt(jnp.mean(value * value, axis=-1, keepdims=True) + EPS)
        normed[rows, :] = (value * scale * gain[...]).astype(BF)
        scales[rows, :] = jnp.broadcast_to(scale, (16, 128))
        return carry

    lax.fori_loop(0, 8, text_rows, 0)
    for chunk in ORDER:
        ring_sum.relay(chunk)
    for number, part in enumerate(rings):
        first, second = part[2].relay()
        forward(first, number * 7 + 1)
        forward(second, number * 7 + 2)
    for number, part in enumerate(rings):
        for arrival in (2, 3):
            forward(part[2].arrived(arrival), number * 7 + 1 + arrival)
    for chunk in ORDER:
        visual_out[:, pl.ds(chunk * width, width)] = ring_sum.total(chunk).astype(BF)
    for step in range(2):
        rows = pl.ds(step * 16, 16)
        value = visual_out[rows, :].astype(F32)
        scale = lax.rsqrt(jnp.mean(value * value, axis=-1, keepdims=True) + EPS)
        normed[pl.ds(128 + step * 16, 16), :] = (value * scale * gain[...]).astype(BF)
        scales[pl.ds(128 + step * 16, 16), :] = jnp.broadcast_to(scale, (16, 128))
    for number, part in enumerate(rings):
        for arrival in (4, 5):
            forward(part[2].arrived(arrival), number * 7 + 1 + arrival)
    for copy in forwards:
        copy.wait_recv()
    out = pltpu.make_async_copy(weight, weight_out, load.at[5])
    out.start()
    acc[...] = jnp.zeros_like(acc)

    def project(step, carry):
        columns = pl.ds(pl.multiple_of(step * 512, 512), 512)
        block = weight[pl.ds(step * 4, 4)].reshape(512, 1024)
        acc[...] += jnp.dot(normed[:, columns], block, preferred_element_type=F32)
        return carry

    lax.fori_loop(0, 16, project, 0)
    text_pairs[...] = acc[pl.ds(0, 128), :].astype(BF)
    mine = acc[pl.ds(128, 32), :].astype(BF)
    visual_pairs[...] = mine
    picking = (lax.broadcasted_iota(jnp.int32, (128, 32), 0) == slot_of[...]).astype(F32).astype(BF)
    outgoing[:, :, pl.ds(0, 1024)] = jnp.dot(picking, mine, preferred_element_type=F32).astype(BF).reshape(8, 16, 1024)
    outgoing[:, :, pl.ds(1024, 128)] = jnp.dot(picking, row_of[...], preferred_element_type=F32).astype(BF).reshape(8, 16, 128)
    for part in rings:
        for ring in part:
            ring.finish()
    for copy in forwards:
        copy.wait_send()
    for chunk in ORDER:
        swaps[chunk].wait_send()
    ring_sum.finish()
    out.wait()


def first_call(patches, vit_gain, up, down, text, gain, kv, slot_of, row_of):
    shape = jax.ShapeDtypeStruct
    dma = pltpu.SemaphoreType.DMA
    return pl.pallas_call(
        first_kernel,
        out_shape=(
            shape((64, 2, 64, 1024), BF), shape((8, 16, 1152), BF), shape((128, 1024), BF), shape((32, 1024), BF),
            shape((32, 8192), BF), shape((160, 128), F32),
        ),
        in_specs=[ANY, VM, ANY, ANY, ANY, VM, ANY, VM, VM],
        out_specs=(ANY, VM, VM, VM, VM, VM),
        scratch_shapes=[
            pltpu.VMEM((64, 2, 64, 1024), BF), pltpu.VMEM((256, 5120), BF), pltpu.VMEM((5120, 384), BF),
            pltpu.VMEM((384, 8192), BF), pltpu.VMEM((128, 8192), BF), pltpu.VMEM((160, 8192), BF), pltpu.VMEM((256, 384), BF),
            pltpu.VMEM((4, 2, 32, 8192), BF), pltpu.VMEM((4, 32, 8192), BF), pltpu.VMEM((4, 32, 8192), BF),
            pltpu.VMEM((4, 32, 2048), BF), pltpu.VMEM((4, 32, 2048), BF), pltpu.VMEM((4, 32, 2048), BF),
            pltpu.VMEM((160, 1024), F32), pltpu.VMEM((256, 384), F32),
            dma((6,)), dma((54,)), dma((54,)), dma((21,)), dma((21,)), dma((4,)), dma((4,)), dma((12,)), dma((12,)),
        ],
        compiler_params=pltpu.CompilerParams(collective_id=1, has_side_effects=True, vmem_limit_bytes=62 * 2**20),
        name="merge_and_project",
    )(patches, vit_gain, up, down, text, gain, kv, slot_of, row_of)


def exchange_kernel(
    outgoing, text_pairs, pairs, placing, marked,
    landed, turned, arrived, load, ctx_send, ctx_recv, dp_send, dp_recv, send, recv, forward_send, forward_recv,
):
    at = place()
    dp, ctx = lax.axis_index("dp"), lax.axis_index("ctx")
    k, y = at["k"], at["y"]
    greet([(dp, lax.rem(ctx + by, 8)) for by in range(1, 8)] + [(lax.rem(dp + by, 16), ctx) for by in range(1, 16)])
    own = pltpu.make_async_copy(outgoing.at[ctx], landed.at[ctx], load.at[0])
    own.start()
    copies = []
    for by in range(1, 8):
        to = lax.rem(ctx + by, 8)
        copy = remote(outgoing.at[to], landed.at[ctx], ctx_send.at[by - 1], ctx_recv.at[by - 1], (dp, to))
        copy.start()
        copies.append(copy)
    own.wait()
    for by in range(1, 8):
        source = lax.rem(ctx - by + 8, 8)
        remote(landed.at[source], landed.at[source], ctx_send.at[by - 1], ctx_recv.at[by - 1], (dp, source)).wait_recv()
    row = lax.broadcasted_iota(jnp.int32, (128, 128), 0)
    turn = (lax.broadcasted_iota(jnp.int32, (128, 128), 1) == (row % 8) * 16 + row // 8).astype(F32).astype(BF)
    turned[...] = jnp.dot(turn, landed[...].reshape(128, 1152), preferred_element_type=F32).reshape(16, 8, 1152).astype(BF)
    own = pltpu.make_async_copy(turned.at[dp], arrived.at[dp], load.at[1])
    own.start()
    for by in range(1, 16):
        to = lax.rem(dp + by, 16)
        copy = remote(turned.at[to], arrived.at[dp], dp_send.at[by - 1], dp_recv.at[by - 1], (to, ctx))
        copy.start()
        copies.append(copy)
    own.wait()
    for by in range(1, 16):
        source = lax.rem(dp - by + 16, 16)
        remote(arrived.at[source], arrived.at[source], dp_send.at[by - 1], dp_recv.at[by - 1], (source, ctx)).wait_recv()
    rows = arrived[:, :, pl.ds(1024, 128)].astype(F32).reshape(128, 128)
    lane = lax.broadcasted_iota(jnp.int32, (128, 128), 1).astype(F32) + 1.0
    places = (rows == lane).astype(F32).astype(BF)
    placing[...] = places
    contract = (((0,), (0,)), ((), ()))
    values = arrived[:, :, pl.ds(0, 1024)].astype(F32).reshape(128, 1024).astype(BF)
    placed = lax.dot_general(places, values, contract, preferred_element_type=F32)
    mark = lax.dot_general(places, jnp.ones((128, 128), BF), contract, preferred_element_type=F32)
    marked[...] = mark
    pairs[y, k] = jnp.where(mark[:, :1] > 0.5, placed, text_pairs[...].astype(F32)).astype(BF)

    partner = device(shifted(at, "k", 1))
    ring = Ring(at, "y", lambda coordinate, half: pairs.at[coordinate, k, pl.ds(64 * half, 64)], send, recv, 0)
    forwards = []

    def forward(ref, number):
        copy = remote(ref, ref, forward_send.at[number], forward_recv.at[number], partner)
        copy.start()
        forwards.append(copy)

    ring.start()
    forward(pairs.at[y, k], 0)
    first, second = ring.relay()
    forward(first, 1)
    forward(second, 2)
    for number in (2, 3, 4, 5):
        forward(ring.arrived(number), number + 1)
    for copy in forwards:
        copy.wait()
    for copy in copies:
        copy.wait_send()
    ring.finish()


def exchange_call(outgoing, text_pairs):
    shape = jax.ShapeDtypeStruct
    dma = pltpu.SemaphoreType.DMA
    return pl.pallas_call(
        exchange_kernel,
        out_shape=(shape((4, 2, 128, 1024), BF), shape((128, 128), BF), shape((128, 128), F32)),
        in_specs=[VM, VM],
        out_specs=(VM, VM, VM),
        scratch_shapes=[
            pltpu.VMEM((8, 16, 1152), BF), pltpu.VMEM((16, 8, 1152), BF), pltpu.VMEM((16, 8, 1152), BF),
            dma((2,)), dma((7,)), dma((7,)), dma((15,)), dma((15,)), dma((6,)), dma((6,)), dma((7,)), dma((7,)),
        ],
        compiler_params=pltpu.CompilerParams(collective_id=2, has_side_effects=True),
        name="exchange_pairs",
    )(outgoing, text_pairs)


WINDOW = 640


def attend_kernel(assign, own, pairs_hbm, docs, queries, upstream, attn_out, q_grad, pair_grads, held, turned, load):
    head = pl.program_id(0)

    @pl.when(head == 0)
    def _():
        for block in range(16):
            pltpu.make_async_copy(pairs_hbm.at[block], held.at[assign[block]], load.at[block]).start()
        for block in range(16):
            pltpu.make_async_copy(pairs_hbm.at[block], held.at[assign[block]], load.at[block]).wait()

    labels = docs[...]
    starts = [jnp.sum((labels < d).astype(F32)).astype(jnp.int32) for d in (1, 2, 3)]
    key_columns = pl.ds(pl.multiple_of(head * HD, HD), HD)
    value_columns = pl.ds(pl.multiple_of(KVH * HD + head * HD, HD), HD)
    turned[...] = jnp.zeros_like(turned)
    score_scale = HD**-0.5
    outer = (((0,), (0,)), ((), ()))
    inner = (((1,), (1,)), ((), ()))
    for half in range(2):
        position = assign[own[0] * 2 + half]
        low = jnp.maximum(position // 2 - 4, 0)
        rows = pl.ds(half * 64, 64)
        query = jnp.concatenate([queries[rows, g * HD : (g + 1) * HD] for g in range(GROUP)], axis=0)
        grad = jnp.concatenate([upstream[rows, g * HD : (g + 1) * HD] for g in range(GROUP)], axis=0)
        blocks = pl.ds(low * 2, WINDOW // 64)
        keys = held[blocks, :, key_columns].reshape(WINDOW, HD)
        values = held[blocks, :, value_columns].reshape(WINDOW, HD)
        query_at = position * 64 + lax.broadcasted_iota(jnp.int32, (64, WINDOW), 0)
        key_at = low * 128 + lax.broadcasted_iota(jnp.int32, (64, WINDOW), 1)
        begin = jnp.zeros((64, WINDOW), jnp.int32)
        for start in starts:
            begin = jnp.where(query_at >= start, start, begin)
        allowed = (key_at <= query_at) & (key_at >= begin)
        scores = lax.dot_general(query, keys, inner, preferred_element_type=F32).reshape(GROUP, 64, WINDOW)
        scores = jnp.where(allowed[None], scores * (score_scale * math.log2(math.e)), -1e30)
        weights = jnp.exp2(scores - jnp.max(scores, axis=-1, keepdims=True))
        weights = weights * (1.0 / jnp.sum(weights, axis=-1, keepdims=True))
        weights = weights.reshape(GROUP * 64, WINDOW)
        light = weights.astype(BF)
        output = jnp.dot(light, values, preferred_element_type=F32)
        weight_grad = lax.dot_general(grad, values, inner, preferred_element_type=F32)
        inner_sum = jnp.sum(weights * weight_grad, axis=-1, keepdims=True)
        score_grad = (weights * (weight_grad - inner_sum)).astype(BF)
        query_grad = jnp.dot(score_grad, keys, preferred_element_type=F32) * score_scale
        window = pl.ds(pl.multiple_of(low * 128, 128), WINDOW)
        turned[0, :, window] += lax.dot_general(query, score_grad, outer, preferred_element_type=F32)
        turned[1, :, window] += lax.dot_general(grad, light, outer, preferred_element_type=F32)
        for g in range(GROUP):
            attn_out[rows, g * HD : (g + 1) * HD] = output[g * 64 : (g + 1) * 64].astype(BF)
            q_grad[rows, g * HD : (g + 1) * HD] = query_grad[g * 64 : (g + 1) * 64].astype(BF)
    upright = (turned[0] * score_scale).T.reshape(16, 64, HD).astype(BF)
    straight = turned[1].T.reshape(16, 64, HD).astype(BF)
    held[:, :, key_columns] = upright
    held[:, :, value_columns] = straight
    for block in range(16):
        pair_grads[block, :, key_columns] = held[assign[block], :, key_columns]
        pair_grads[block, :, value_columns] = held[assign[block], :, value_columns]


def attend_call(assign, own, pairs, docs, queries, upstream):
    shape = jax.ShapeDtypeStruct
    by_head = pl.BlockSpec((128, GROUP * HD), lambda head, *_: (0, head))
    return pl.pallas_call(
        attend_kernel,
        out_shape=(shape((128, 4096), BF), shape((128, 4096), BF), shape((16, 64, 1024), BF)),
        grid_spec=pltpu.PrefetchScalarGridSpec(
            num_scalar_prefetch=2,
            grid=(KVH,),
            in_specs=[ANY, pl.BlockSpec((1, 1024), lambda head, *_: (0, 0)), by_head, by_head],
            out_specs=(by_head, by_head, pl.BlockSpec((16, 64, 1024), lambda head, *_: (0, 0, 0))),
            scratch_shapes=[pltpu.VMEM((16, 64, 1024), BF), pltpu.VMEM((2, HD, 1024), F32), pltpu.SemaphoreType.DMA((16,))],
        ),
        compiler_params=pltpu.CompilerParams(vmem_limit_bytes=56 * 2**20),
        name="attend",
    )(assign, own, pairs, docs, queries, upstream)


def return_kernel(
    grads, placing, slot_of, own_grad, visual_grad,
    from_partner, sums, far, plain, through, leaving, landed, turned, arrived,
    load, pair_send, pair_recv, sum_send, sum_recv, dp_send, dp_recv, ctx_send, ctx_recv,
):
    at = place()
    dp, ctx = lax.axis_index("dp"), lax.axis_index("ctx")
    k, y = at["k"], at["y"]
    greet([(dp, lax.rem(ctx + by, 8)) for by in range(1, 8)] + [(lax.rem(dp + by, 16), ctx) for by in range(1, 16)])
    partner = device(shifted(at, "k", 1))
    width = 256
    swaps = {}
    for chunk in ORDER:
        columns = pl.ds(chunk * width, width)
        swaps[chunk] = remote(
            grads.at[:, 1 - k, :, columns], from_partner.at[:, :, columns], pair_send.at[chunk], pair_recv.at[chunk], partner
        )
        swaps[chunk].start()
    ring_sum = RingSum(at, sums, far, plain, through, 4, sum_send, sum_recv)
    for chunk in ORDER:
        swaps[chunk].wait_recv()
        columns = pl.ds(chunk * width, width)
        for block in range(4):
            mine = grads[block, pl.ds(k, 1), :, columns].reshape(128, width)
            sums[block, :, columns] = (mine.astype(F32) + from_partner[block, :, columns].astype(F32)).astype(BF)
        ring_sum.start(chunk)
    for chunk in ORDER:
        ring_sum.relay(chunk)
    for chunk in ORDER:
        own_grad[:, pl.ds(chunk * width, width)] = ring_sum.total(chunk).astype(BF)
    leaving[...] = jnp.dot(placing[...], own_grad[...], preferred_element_type=F32).reshape(16, 8, 1024).astype(BF)
    own = pltpu.make_async_copy(leaving.at[dp], landed.at[dp], load.at[0])
    own.start()
    copies = []
    for by in range(1, 16):
        to = lax.rem(dp + by, 16)
        copy = remote(leaving.at[to], landed.at[dp], dp_send.at[by - 1], dp_recv.at[by - 1], (to, ctx))
        copy.start()
        copies.append(copy)
    own.wait()
    for by in range(1, 16):
        source = lax.rem(dp - by + 16, 16)
        remote(landed.at[source], landed.at[source], dp_send.at[by - 1], dp_recv.at[by - 1], (source, ctx)).wait_recv()
    row = lax.broadcasted_iota(jnp.int32, (128, 128), 0)
    turn = (lax.broadcasted_iota(jnp.int32, (128, 128), 1) == (row % 16) * 8 + row // 16).astype(F32).astype(BF)
    came = landed[...].astype(F32).reshape(128, 1024).astype(BF)
    turned[...] = jnp.dot(turn, came, preferred_element_type=F32).astype(BF).reshape(8, 16, 1024)
    own = pltpu.make_async_copy(turned.at[ctx], arrived.at[ctx], load.at[1])
    own.start()
    for by in range(1, 8):
        to = lax.rem(ctx + by, 8)
        copy = remote(turned.at[to], arrived.at[ctx], ctx_send.at[by - 1], ctx_recv.at[by - 1], (dp, to))
        copy.start()
        copies.append(copy)
    own.wait()
    for by in range(1, 8):
        source = lax.rem(ctx - by + 8, 8)
        remote(arrived.at[source], arrived.at[source], ctx_send.at[by - 1], ctx_recv.at[by - 1], (dp, source)).wait_recv()
    picking = (slot_of[...] == lax.broadcasted_iota(jnp.int32, (32, 128), 1)).astype(F32).astype(BF)
    visual_grad[...] = jnp.dot(picking, arrived[...].reshape(128, 1024), preferred_element_type=F32).astype(BF)
    for copy in copies:
        copy.wait_send()
    for chunk in ORDER:
        swaps[chunk].wait_send()
    ring_sum.finish()


def return_call(grads, placing, slot_of):
    shape = jax.ShapeDtypeStruct
    dma = pltpu.SemaphoreType.DMA
    return pl.pallas_call(
        return_kernel,
        out_shape=(shape((128, 1024), BF), shape((32, 1024), BF)),
        in_specs=[VM, VM, VM],
        out_specs=(VM, VM),
        scratch_shapes=[
            pltpu.VMEM((4, 128, 1024), BF), pltpu.VMEM((4, 128, 1024), BF),
            pltpu.VMEM((4, 128, 256), BF), pltpu.VMEM((4, 128, 256), BF), pltpu.VMEM((4, 128, 256), BF),
            pltpu.VMEM((16, 8, 1024), BF), pltpu.VMEM((16, 8, 1024), BF), pltpu.VMEM((8, 16, 1024), BF), pltpu.VMEM((8, 16, 1024), BF),
            dma((2,)), dma((4,)), dma((4,)), dma((12,)), dma((12,)), dma((15,)), dma((15,)), dma((7,)), dma((7,)),
        ],
        compiler_params=pltpu.CompilerParams(collective_id=3, has_side_effects=True),
        name="return_grads",
    )(grads, placing, slot_of)


def final_kernel(
    own_grad, visual_pair_grad, text_pairs, visual_pairs, weight, text, visual, gain, scales, marked, hidden_grad, visual_grad
):
    contract = (((1,), (1,)), ((), ()))
    block = weight[...]
    gains = gain[...]

    def through(grad, pair, value, scale):
        mean = jnp.sum(grad.astype(F32) * pair.astype(F32), axis=-1, keepdims=True) * (1.0 / 8192.0)
        normed_grad = lax.dot_general(grad, block, contract, preferred_element_type=F32)
        return scale * (gains * normed_grad) - value.astype(F32) * (scale * scale * mean)

    full = through(own_grad[...], text_pairs[...], text[...], scales[0:128, 0:1])
    hidden_grad[...] = jnp.where(marked[:, 0:1] > 0.5, 0.0, full).astype(BF)
    visual_grad[...] = through(visual_pair_grad[...], visual_pairs[...], visual[...], scales[128:160, 0:1]).astype(BF)


def final_call(own_grad, visual_pair_grad, text_pairs, visual_pairs, weight, text, visual, gain, scales, marked):
    shape = jax.ShapeDtypeStruct
    tile = 1024

    def whole(*dims):
        return pl.BlockSpec(dims, lambda i: (0,) * len(dims))

    return pl.pallas_call(
        final_kernel,
        out_shape=(shape((128, 8192), BF), shape((32, 8192), BF)),
        grid=(8192 // tile,),
        in_specs=[
            whole(128, 1024), whole(32, 1024), whole(128, 1024), whole(32, 1024),
            pl.BlockSpec((tile, 1024), lambda i: (i, 0)), pl.BlockSpec((128, tile), lambda i: (0, i)),
            pl.BlockSpec((32, tile), lambda i: (0, i)), pl.BlockSpec((1, tile), lambda i: (0, i)),
            whole(160, 128), whole(128, 128),
        ],
        out_specs=(pl.BlockSpec((128, tile), lambda i: (0, i)), pl.BlockSpec((32, tile), lambda i: (0, i))),
        compiler_params=pltpu.CompilerParams(vmem_limit_bytes=48 * 2**20),
        name="through_norm",
    )(own_grad, visual_pair_grad, text_pairs, visual_pairs, weight, text, visual, gain, scales, marked)


def local(patches, vit_gain, merge_up, merge_down, dest, text, norm_gain, kv_weight, queries, out_grad, assign, docs):
    target = dest // 128
    slot = (target % 8) * 16 + target // 8
    row_of = jnp.broadcast_to((dest % 128 + 1).astype(BF)[:, None], (32, 128))
    gain = norm_gain.reshape(1, 8192)
    weight, outgoing, text_pairs, visual_pairs, visual, scales = first_call(
        patches, vit_gain.reshape(1, 1280), merge_up, merge_down, text[0], gain, kv_weight, slot.reshape(1, 32), row_of
    )
    pairs, placing, marked = exchange_call(outgoing, text_pairs)
    own = lax.axis_index("ctx").astype(jnp.int32).reshape(1)
    attention, query_grad, pair_grads = attend_call(assign, own, pairs.reshape(16, 64, 1024), docs, queries[0], out_grad[0])
    own_grad, visual_pair_grad = return_call(
        pair_grads.reshape(4, 2, 128, 1024), placing, jnp.broadcast_to(slot[:, None], (32, 128))
    )
    hidden_grad, visual_grad = final_call(
        own_grad, visual_pair_grad, text_pairs, visual_pairs, weight.reshape(8192, 1024), text[0], visual, gain, scales, marked
    )
    return attention[None], query_grad[None], hidden_grad[None], visual_grad


def solution(mesh):
    placed = (
        P("dp", None),
        P(),
        P(None, "ctx"),
        P("ctx", None),
        P(("dp", "ctx")),
        P("dp", "ctx", None),
        P(),
        P(("dp", "ctx"), None),
        P("dp", "ctx", None),
        P("dp", "ctx", None),
        P(),
        P("dp", None),
    )
    return jax.shard_map(
        local,
        mesh=mesh,
        in_specs=placed,
        out_specs=(P("dp", "ctx", None), P("dp", "ctx", None), P("dp", "ctx", None), P(("dp", "ctx"), None)),
        check_vma=False,
    )
```

profile of v0, /device:TPU:1, one launch (start us, length us, event | category | flops | bytes accessed | tf_op | source)
XLA Modules:
  0.0 171.8 jit_solution(1953737050325574635)
XLA Ops:
  0.6 1.2 fusion.3
  1.8 0.7 broadcast_in_dim.10.row_of
  2.5 1.3 reshape.32.vit_gain
  3.8 71.2 %merge_and_project.1 = (bf16[64,2,64,1024]{3,2,1,0:T(8,128)(2,1)}, bf16[8,16,1152]{2,1,0:T(8,128)(2,1)}, bf16[128,1024]{1,0:T(8,128)(2,1)}, bf16[32,1024]{1,0:T(...) custom-call(bf16[256,5120]{1,0:T(8,128)(2,1)} %patches_hbm.1, f32[1,1280]{1,0:T(1,128)} %reshape.32.vit_gain, ...), custom_call_target="tpu_custom_call" | custom-call | tf_op jit(solution)/shard_map/merge_and_project/pallas_call | solution.py:318
  75.0 0.0 copy-start.9
  75.0 29.6 %exchange_pairs.1 = (bf16[4,2,128,1024]{3,2,1,0:T(8,128)(2,1)}, bf16[128,128]{1,0:T(8,128)(2,1)}, f32[128,128]{1,0:T(8,128)}) custom-call(bf16[8,16,1152]{2,1,0:T(8,128)(2,1)} %get-tuple-element.20.outgoing, bf16[128,1024]{1,0:T(8,128)(2,1)} %get-tuple-element.21.text_pairs), custom_call_target="tpu_custom_call" | custom-call | tf_op jit(solution)/shard_map/exchange_pairs/pallas_call | solution.py:410
  104.6 0.0 copy-start
  104.6 0.0 copy-start.1
  104.7 0.0 copy-start.2
  104.7 0.0 copy-start.4
  104.7 0.0 copy-start.5
  104.7 0.0 copy-start.6
  104.7 0.0 copy-start.7
  104.7 19.8 %attend.1 = (bf16[128,4096]{1,0:T(8,128)(2,1)}, bf16[128,4096]{1,0:T(8,128)(2,1)}, bf16[16,64,1024]{2,1,0:T(8,128)(2,1)}) custom-call(s32[16]{0:T(128)} %assign.1, s32[1]{0:T(128)} %bitcast.own, bf16[16,64,1024]{2,1,0:T(8,128)(2,1)} %bitcast.17, s32[1,1024]{1,0:T(1,128)} %docs.1, bf16[128,4096]{1,0:T(8,128)(2,1)} %bitcast.19, bf16[128,4096]{1,0:T(8,128)(2,1)} %bitcast.20), custom_call_target="tpu_custom_call" | custom-call | tf_op jit(solution)/shard_map/attend/pallas_call | solution.py:489
  124.5 0.0 copy-done.9
  124.5 0.7 broadcast_in_dim.24.slot_of
  125.2 30.4 %return_grads.1 = (bf16[128,1024]{1,0:T(8,128)(2,1)}, bf16[32,1024]{1,0:T(8,128)(2,1)}) custom-call(bf16[4,2,128,1024]{3,2,1,0:T(8,128)(2,1)} %bitcast.18, bf16[128,128]{1,0:T(8,128)(2,1)} %get-tuple-element.26.placing, s32[32,128]{1,0:T(8,128)} %broadcast_in_dim.24.slot_of), custom_call_target="tpu_custom_call" | custom-call | tf_op jit(solution)/shard_map/return_grads/pallas_call | solution.py:574
  155.5 0.0 copy-done
  155.5 0.0 copy-done.1
  155.5 0.0 copy-done.2
  155.6 0.0 copy-done.4
  155.6 0.0 copy-done.5
  155.6 0.0 copy-done.6
  155.6 0.0 copy-done.7
  155.6 0.0 copy-start.3
  155.6 0.9 copy-done.3
  156.5 0.0 copy-start.8
  156.6 0.8 copy-done.8
  157.4 14.4 %through_norm.1 = (bf16[128,8192]{1,0:T(8,128)(2,1)}, bf16[32,8192]{1,0:T(8,128)(2,1)}) custom-call(bf16[128,1024]{1,0:T(8,128)(2,1)S(1)} %copy-done.3, bf16[32,1024]{1,0:T(8,128)(2,1)S(1)} %copy-done.8, bf16[128,1024]{1,0:T(8,128)(2,1)S(1)} %copy-done.1, bf16[32,1024]{1,0:T(8,128)(2,1)S(1)} %copy-done.6, bf16[8192,1024]{1,0:T(8,128)(2,1)} %bitcast.16, ...), custom_call_target="tpu_custom_call" | custom-call | tf_op jit(solution)/shard_map/through_norm/pallas_call | solution.py:614
Async XLA Ops:
  75.0 49.5 %copy-start.9 = (s32[32]{0:T(128)S(1)}, s32[32]{0:T(128)}, u32[]{:S(2)}) copy-start(s32[32]{0:T(128)} %get-tuple-element.37) | copy-start | bytes 388
  104.6 50.9 %copy-start = (bf16[1,128,8192]{2,1,0:T(8,128)(2,1)S(1)}, bf16[1,128,8192]{2,1,0:T(8,128)(2,1)}, u32[]{:S(2)}) copy-start(bf16[1,128,8192]{2,1,0:T(8,128)(2,1)} %param.17) | copy-start | bytes 6291460
  104.6 50.9 %copy-start.1 = (bf16[128,1024]{1,0:T(8,128)(2,1)S(1)}, bf16[128,1024]{1,0:T(8,128)(2,1)}, u32[]{:S(2)}) copy-start(bf16[128,1024]{1,0:T(8,128)(2,1)} %get-tuple-element.21.text_pairs) | copy-start | bytes 786436
  104.7 50.9 %copy-start.2 = (bf16[32,8192]{1,0:T(8,128)(2,1)S(1)}, bf16[32,8192]{1,0:T(8,128)(2,1)}, u32[]{:S(2)}) copy-start(bf16[32,8192]{1,0:T(8,128)(2,1)} %get-tuple-element.31.visual) | copy-start | bytes 1572868
  104.7 50.9 %copy-start.4 = (f32[8192]{0:T(1024)S(1)}, f32[8192]{0:T(1024)}, u32[]{:S(2)}) copy-start(f32[8192]{0:T(1024)} %param.18) | copy-start | bytes 98308
  104.7 50.9 %copy-start.5 = (f32[160,128]{1,0:T(8,128)S(1)}, f32[160,128]{1,0:T(8,128)}, u32[]{:S(2)}) copy-start(f32[160,128]{1,0:T(8,128)} %get-tuple-element.32.scales) | copy-start | bytes 245764
  104.7 50.9 %copy-start.6 = (bf16[32,1024]{1,0:T(8,128)(2,1)S(1)}, bf16[32,1024]{1,0:T(8,128)(2,1)}, u32[]{:S(2)}) copy-start(bf16[32,1024]{1,0:T(8,128)(2,1)} %get-tuple-element.29.visual_pairs) | copy-start | bytes 196612
  104.7 50.9 %copy-start.7 = (f32[128,128]{1,0:T(8,128)S(1)}, f32[128,128]{1,0:T(8,128)}, u32[]{:S(2)}) copy-start(f32[128,128]{1,0:T(8,128)} %get-tuple-element.33.marked) | copy-start | bytes 196612
  155.6 1.0 copy-start.3
  156.5 0.8 copy-start.8
where the time goes:
time: 172 us
  Pallas kernels  165 us (96%)
  local copies, waits for them, and re-layouts  4.46 us (3%)
    pallas_call x1, Pallas kernels, first_call(): pl.pallas_call(first_kernel, out_shape=(shape((64, 2, 64, 1024), BF), sha...  71.2 us
    pallas_call x1, Pallas kernels, return_call(): pl.pallas_call(return_kernel, out_shape=(shape((128, 1024), BF), shape((3...  30.4 us
    pallas_call x1, Pallas kernels, exchange_call(): pl.pallas_call(exchange_kernel, out_shape=(shape((4, 2, 128, 1024), BF),...  29.6 us
    pallas_call x1, Pallas kernels, attend_call(): pl.pallas_call(attend_kernel, out_shape=(shape((128, 4096), BF), shape((1...  19.8 us
    pallas_call x1, Pallas kernels, final_call(): pl.pallas_call(final_kernel, out_shape=(shape((128, 8192), BF), shape((32...  14.4 us

commit v1 on v0

--- a/solution.py
+++ b/solution.py
@@ -47,6 +47,11 @@
     pl.semaphore_wait(barrier, len(devices))
 
 
+def upright(row):
+    same = lax.broadcasted_iota(jnp.int32, (32, 32), 0) == lax.broadcasted_iota(jnp.int32, (32, 32), 1)
+    return jnp.sum(jnp.where(same, jnp.broadcast_to(row, (32, 32)), 0).astype(F32), axis=1, keepdims=True)
+
+
 class Ring:
     def __init__(self, at, axis, slab, send, recv, base):
         self.at, self.axis, self.slab, self.send, self.recv, self.base = at, axis, slab, send, recv, base
@@ -132,15 +137,15 @@
             copy.wait_send()
 
 
-PARTS = ((0, 384, "yzx"), (384, 384, "yxz"), (768, 256, "xzy"))
+PARTS = ((0, 384, "yzx"), (384, 384, "xyz"), (768, 256, "zxy"))
 ORDER = (0, 2, 1, 3)
 
 
 def first_kernel(
-    patches_hbm, vit_gain, up_hbm, down_hbm, text_hbm, gain, kv_hbm, slot_of, row_of,
+    patches_hbm, vit_gain, up_hbm, down_hbm, text_hbm, gain, kv_hbm, dest,
     weight_out, outgoing, text_pairs, visual_pairs, visual_out, scales,
     weight, patches, up, down, text, normed, hidden, partial, from_partner, sums, far, plain, through, acc, inner,
-    load, send, recv, forward_send, forward_recv, pair_send, pair_recv, sum_send, sum_recv,
+    load, send, recv, forward_send, forward_recv, pair_send, pair_recv, sum_send, sum_recv, store,
 ):
     at = place()
     k, y = at["k"], at["y"]
@@ -160,8 +165,7 @@
         def slab(coordinate, half):
             cut = {name: (pl.ds(0, 4) if name in axes_done else pl.ds(at[name], 1)) for name in "xyz"}
             cut[axis] = pl.ds(coordinate, 1)
-            view = weight.reshape(4, 4, 4, 2, 64, 1024) if False else weight6
-            return view.at[cut["x"], cut["z"], cut["y"], k, pl.ds(32 * half, 32), pl.ds(first, count)]
+            return weight6.at[cut["x"], cut["z"], cut["y"], k, pl.ds(32 * half, 32), pl.ds(first, count)]
 
         return slab
 
@@ -173,18 +177,18 @@
         ]
         for part, (first, count, order) in enumerate(PARTS)
     ]
-    forwards = []
+    forwards = [{} for _ in PARTS]
 
     def forward(ref, number):
         copy = remote(ref, ref, forward_send.at[number], forward_recv.at[number], partner)
         copy.start()
-        forwards.append(copy)
+        forwards[number // 7][number % 7] = copy
 
     for part in rings:
         part[0].start()
 
     loads[0].wait()
-    vg = vit_gain[...]
+    vg = vit_gain[...].reshape(1, 1280)
 
     def norm_rows(step, carry):
         rows = pl.ds(pl.multiple_of(step * 16, 16), 16)
@@ -279,49 +283,69 @@
         scale = lax.rsqrt(jnp.mean(value * value, axis=-1, keepdims=True) + EPS)
         normed[pl.ds(128 + step * 16, 16), :] = (value * scale * gain[...]).astype(BF)
         scales[pl.ds(128 + step * 16, 16), :] = jnp.broadcast_to(scale, (16, 128))
+    stores = []
+    out6 = weight_out.reshape(4, 4, 4, 2, 64, 1024)
+
+    def keep(step, numbers):
+        for number, (first, count, order) in enumerate(PARTS):
+            for each in numbers:
+                forwards[number][each].wait_recv()
+            spot = shifted(at, order[2], step)[order[2]]
+            cut = {name: (pl.ds(spot, 1) if name == order[2] else pl.ds(0, 4)) for name in "xyz"}
+            boxes = [
+                ref.at[cut["x"], cut["z"], cut["y"], :, :, pl.ds(first, count)] for ref in (weight6, out6)
+            ]
+            copy = pltpu.make_async_copy(boxes[0], boxes[1], store.at[len(stores)])
+            copy.start()
+            stores.append(copy)
+
+    keep(0, (0,))
     for number, part in enumerate(rings):
         for arrival in (4, 5):
             forward(part[2].arrived(arrival), number * 7 + 1 + arrival)
-    for copy in forwards:
-        copy.wait_recv()
-    out = pltpu.make_async_copy(weight, weight_out, load.at[5])
-    out.start()
+    keep(-1, (1, 3))
+    keep(1, (2, 4))
+    keep(2, (5, 6))
     acc[...] = jnp.zeros_like(acc)
 
     def project(step, carry):
-        columns = pl.ds(pl.multiple_of(step * 512, 512), 512)
-        block = weight[pl.ds(step * 4, 4)].reshape(512, 1024)
+        columns = pl.ds(pl.multiple_of(step * 2048, 2048), 2048)
+        block = weight[pl.ds(step * 16, 16)].reshape(2048, 1024)
         acc[...] += jnp.dot(normed[:, columns], block, preferred_element_type=F32)
         return carry
 
-    lax.fori_loop(0, 16, project, 0)
+    lax.fori_loop(0, 4, project, 0)
     text_pairs[...] = acc[pl.ds(0, 128), :].astype(BF)
     mine = acc[pl.ds(128, 32), :].astype(BF)
     visual_pairs[...] = mine
-    picking = (lax.broadcasted_iota(jnp.int32, (128, 32), 0) == slot_of[...]).astype(F32).astype(BF)
-    outgoing[:, :, pl.ds(0, 1024)] = jnp.dot(picking, mine, preferred_element_type=F32).astype(BF).reshape(8, 16, 1024)
-    outgoing[:, :, pl.ds(1024, 128)] = jnp.dot(picking, row_of[...], preferred_element_type=F32).astype(BF).reshape(8, 16, 128)
+    entry = dest[...].reshape(1, 32)
+    row_of = jnp.broadcast_to(upright(entry % 128 + 1), (32, 128)).astype(BF)
+    picking = (lax.broadcasted_iota(jnp.int32, (128, 32), 0) == entry // 128).astype(F32).astype(BF)
+    outgoing[:, :, pl.ds(0, 1024)] = jnp.dot(picking, mine, preferred_element_type=F32).reshape(16, 8, 1024).astype(BF)
+    outgoing[:, :, pl.ds(1024, 128)] = jnp.dot(picking, row_of, preferred_element_type=F32).reshape(16, 8, 128).astype(BF)
     for part in rings:
         for ring in part:
             ring.finish()
-    for copy in forwards:
-        copy.wait_send()
+    for part in forwards:
+        for copy in part.values():
+            copy.wait_send()
     for chunk in ORDER:
         swaps[chunk].wait_send()
     ring_sum.finish()
-    out.wait()
-
-
-def first_call(patches, vit_gain, up, down, text, gain, kv, slot_of, row_of):
+    for copy in stores:
+        copy.wait()
+
+
+def first_call(patches, vit_gain, up, down, text, gain, kv, dest):
     shape = jax.ShapeDtypeStruct
     dma = pltpu.SemaphoreType.DMA
     return pl.pallas_call(
         first_kernel,
         out_shape=(
-            shape((64, 2, 64, 1024), BF), shape((8, 16, 1152), BF), shape((128, 1024), BF), shape((32, 1024), BF),
+            shape((64, 2, 64, 1024), BF), shape((16, 8, 1152), BF), shape((128, 1024), BF), shape((32, 1024), BF),
             shape((32, 8192), BF), shape((160, 128), F32),
         ),
-        in_specs=[ANY, VM, ANY, ANY, ANY, VM, ANY, VM, VM],
+        in_specs=[ANY, VM, ANY, ANY, ANY, VM, ANY, VM],
         out_specs=(ANY, VM, VM, VM, VM, VM),
         scratch_shapes=[
             pltpu.VMEM((64, 2, 64, 1024), BF), pltpu.VMEM((256, 5120), BF), pltpu.VMEM((5120, 384), BF),
@@ -329,110 +353,177 @@
             pltpu.VMEM((4, 2, 32, 8192), BF), pltpu.VMEM((4, 32, 8192), BF), pltpu.VMEM((4, 32, 8192), BF),
             pltpu.VMEM((4, 32, 2048), BF), pltpu.VMEM((4, 32, 2048), BF), pltpu.VMEM((4, 32, 2048), BF),
             pltpu.VMEM((160, 1024), F32), pltpu.VMEM((256, 384), F32),
-            dma((6,)), dma((54,)), dma((54,)), dma((21,)), dma((21,)), dma((4,)), dma((4,)), dma((12,)), dma((12,)),
+            dma((6,)), dma((54,)), dma((54,)), dma((21,)), dma((21,)), dma((4,)), dma((4,)), dma((12,)), dma((12,)), dma((12,)),
         ],
         compiler_params=pltpu.CompilerParams(collective_id=1, has_side_effects=True, vmem_limit_bytes=62 * 2**20),
         name="merge_and_project",
-    )(patches, vit_gain, up, down, text, gain, kv, slot_of, row_of)
+    )(patches, vit_gain, up, down, text, gain, kv, dest)
 
 
 def exchange_kernel(
-    outgoing, text_pairs, pairs, placing, marked,
-    landed, turned, arrived, load, ctx_send, ctx_recv, dp_send, dp_recv, send, recv, forward_send, forward_recv,
+    outgoing, text_pairs, weight, text_all, visual_all, placing, marked, weight_t,
+    landed, turned, arrived, block, block_t,
+    load, store, ctx_send, ctx_recv, dp_send, dp_recv, send, recv, forward_send, forward_recv,
 ):
     at = place()
     dp, ctx = lax.axis_index("dp"), lax.axis_index("ctx")
     k, y = at["k"], at["y"]
+    own = pltpu.make_async_copy(text_pairs, text_all.at[y, k], load.at[2])
+    own.start()
+    fetched, stored = [], []
+
+    def fetch(chunk):
+        copy = pltpu.make_async_copy(weight.at[pl.ds(chunk * 1024, 1024)], block.at[chunk % 2], load.at[3 + chunk])
+        copy.start()
+        fetched.append(copy)
+
+    def transpose(chunk):
+        fetched[chunk].wait()
+        if chunk >= 2:
+            stored[chunk - 2].wait()
+
+        def step(i, carry):
+            lanes = pl.ds(pl.multiple_of(i * 128, 128), 128)
+            block_t[chunk % 2, :, lanes] = block[chunk % 2, lanes, :].T
+            return carry
+
+        lax.fori_loop(0, 8, step, 0)
+        copy = pltpu.make_async_copy(block_t.at[chunk % 2], weight_t.at[:, pl.ds(chunk * 1024, 1024)], store.at[chunk])
+        copy.start()
+        stored.append(copy)
+        if chunk + 2 < 8:
+            fetch(chunk + 2)
+
+    fetch(0)
+    fetch(1)
     greet([(dp, lax.rem(ctx + by, 8)) for by in range(1, 8)] + [(lax.rem(dp + by, 16), ctx) for by in range(1, 16)])
-    own = pltpu.make_async_copy(outgoing.at[ctx], landed.at[ctx], load.at[0])
+    partner = device(shifted(at, "k", 1))
+    text_ring = Ring(at, "y", lambda coordinate, half: text_all.at[coordinate, k, pl.ds(64 * half, 64)], send, recv, 0)
+    visual_ring = Ring(at, "y", lambda coordinate, half: visual_all.at[coordinate, k, pl.ds(16 * half, 16)], send, recv, 6)
+    forwards, copies = [], []
+
+    def forward(ref, number):
+        copy = remote(ref, ref, forward_send.at[number], forward_recv.at[number], partner)
+        copy.start()
+        forwards.append(copy)
+
+    for by in range(1, 16):
+        to = lax.rem(dp + by, 16)
+        copy = remote(outgoing.at[to], landed.at[dp], dp_send.at[by - 1], dp_recv.at[by - 1], (to, ctx))
+        copy.start()
+        copies.append(copy)
+    own.wait()
+    text_ring.start()
+    forward(text_all.at[y, k], 0)
+    own = pltpu.make_async_copy(outgoing.at[dp], landed.at[dp], load.at[0])
     own.start()
-    copies = []
+    transpose(0)
+    transpose(1)
+    first, second = text_ring.relay()
+    forward(first, 1)
+    forward(second, 2)
+    own.wait()
+    for by in range(1, 16):
+        source = lax.rem(dp - by + 16, 16)
+        remote(landed.at[source], landed.at[source], dp_send.at[by - 1], dp_recv.at[by - 1], (source, ctx)).wait_recv()
+    row = lax.broadcasted_iota(jnp.int32, (128, 128), 0)
+    turn = (lax.broadcasted_iota(jnp.int32, (128, 128), 1) == (row % 16) * 8 + row // 16).astype(F32).astype(BF)
+    came = landed[...].astype(F32).reshape(128, 1152).astype(BF)
+    turned[...] = jnp.dot(turn, came, preferred_element_type=F32).astype(BF).reshape(8, 16, 1152)
     for by in range(1, 8):
         to = lax.rem(ctx + by, 8)
-        copy = remote(outgoing.at[to], landed.at[ctx], ctx_send.at[by - 1], ctx_recv.at[by - 1], (dp, to))
+        copy = remote(turned.at[to], arrived.at[ctx], ctx_send.at[by - 1], ctx_recv.at[by - 1], (dp, to))
         copy.start()
         copies.append(copy)
+    own = pltpu.make_async_copy(turned.at[ctx], arrived.at[ctx], load.at[1])
+    own.start()
+    transpose(2)
+    transpose(3)
     own.wait()
     for by in range(1, 8):
         source = lax.rem(ctx - by + 8, 8)
-        remote(landed.at[source], landed.at[source], ctx_send.at[by - 1], ctx_recv.at[by - 1], (dp, source)).wait_recv()
-    row = lax.broadcasted_iota(jnp.int32, (128, 128), 0)
-    turn = (lax.broadcasted_iota(jnp.int32, (128, 128), 1) == (row % 8) * 16 + row // 8).astype(F32).astype(BF)
-    turned[...] = jnp.dot(turn, landed[...].reshape(128, 1152), preferred_element_type=F32).reshape(16, 8, 1152).astype(BF)
-    own = pltpu.make_async_copy(turned.at[dp], arrived.at[dp], load.at[1])
-    own.start()
-    for by in range(1, 16):
-        to = lax.rem(dp + by, 16)
-        copy = remote(turned.at[to], arrived.at[dp], dp_send.at[by - 1], dp_recv.at[by - 1], (to, ctx))
-        copy.start()
-        copies.append(copy)
-    own.wait()
-    for by in range(1, 16):
-        source = lax.rem(dp - by + 16, 16)
-        remote(arrived.at[source], arrived.at[source], dp_send.at[by - 1], dp_recv.at[by - 1], (source, ctx)).wait_recv()
+        remote(arrived.at[source], arrived.at[source], ctx_send.at[by - 1], ctx_recv.at[by - 1], (dp, source)).wait_recv()
     rows = arrived[:, :, pl.ds(1024, 128)].astype(F32).reshape(128, 128)
-    lane = lax.broadcasted_iota(jnp.int32, (128, 128), 1).astype(F32) + 1.0
-    places = (rows == lane).astype(F32).astype(BF)
+    lane = lax.broadcasted_iota(jnp.int32, (128, 128), 1).astype(F32)
+    contract = (((0,), (0,)), ((), ()))
+    begin = jnp.min(jnp.where(rows > 0.5, rows, 1000.0), axis=0, keepdims=True)
+    packing = (rows - begin == lane).astype(F32).astype(BF)
+    packed = lax.dot_general(
+        packing, arrived[:, :, pl.ds(0, 1024)].reshape(128, 1024), contract, preferred_element_type=F32
+    )
+    visual_all[y, k, :, pl.ds(0, 1024)] = packed[:32].astype(BF)
+    visual_all[y, k, :, pl.ds(1024, 128)] = jnp.broadcast_to(begin, (32, 128)).astype(BF)
+    visual_ring.start()
+    forward(visual_all.at[y, k], 7)
+    places = (rows == lane + 1.0).astype(F32).astype(BF)
     placing[...] = places
-    contract = (((0,), (0,)), ((), ()))
-    values = arrived[:, :, pl.ds(0, 1024)].astype(F32).reshape(128, 1024).astype(BF)
-    placed = lax.dot_general(places, values, contract, preferred_element_type=F32)
-    mark = lax.dot_general(places, jnp.ones((128, 128), BF), contract, preferred_element_type=F32)
-    marked[...] = mark
-    pairs[y, k] = jnp.where(mark[:, :1] > 0.5, placed, text_pairs[...].astype(F32)).astype(BF)
-
-    partner = device(shifted(at, "k", 1))
-    ring = Ring(at, "y", lambda coordinate, half: pairs.at[coordinate, k, pl.ds(64 * half, 64)], send, recv, 0)
-    forwards = []
-
-    def forward(ref, number):
-        copy = remote(ref, ref, forward_send.at[number], forward_recv.at[number], partner)
-        copy.start()
-        forwards.append(copy)
-
-    ring.start()
-    forward(pairs.at[y, k], 0)
-    first, second = ring.relay()
-    forward(first, 1)
-    forward(second, 2)
+    marked[...] = lax.dot_general(places, jnp.ones((128, 128), BF), contract, preferred_element_type=F32)
+    transpose(4)
     for number in (2, 3, 4, 5):
-        forward(ring.arrived(number), number + 1)
+        forward(text_ring.arrived(number), number + 1)
+    first, second = visual_ring.relay()
+    forward(first, 8)
+    forward(second, 9)
+    transpose(5)
+    for number in (2, 3):
+        forward(visual_ring.arrived(number), number + 8)
+    transpose(6)
+    for number in (4, 5):
+        forward(visual_ring.arrived(number), number + 8)
+    transpose(7)
     for copy in forwards:
         copy.wait()
     for copy in copies:
         copy.wait_send()
-    ring.finish()
-
-
-def exchange_call(outgoing, text_pairs):
+    text_ring.finish()
+    visual_ring.finish()
+    stored[6].wait()
+    stored[7].wait()
+
+
+def exchange_call(outgoing, text_pairs, weight):
     shape = jax.ShapeDtypeStruct
     dma = pltpu.SemaphoreType.DMA
     return pl.pallas_call(
         exchange_kernel,
-        out_shape=(shape((4, 2, 128, 1024), BF), shape((128, 128), BF), shape((128, 128), F32)),
-        in_specs=[VM, VM],
-        out_specs=(VM, VM, VM),
+        out_shape=(
+            shape((4, 2, 128, 1024), BF), shape((4, 2, 32, 1152), BF), shape((128, 128), BF), shape((128, 128), F32),
+            shape((1024, 8192), BF),
+        ),
+        in_specs=[ANY, ANY, ANY],
+        out_specs=(VM, VM, VM, VM, ANY),
         scratch_shapes=[
-            pltpu.VMEM((8, 16, 1152), BF), pltpu.VMEM((16, 8, 1152), BF), pltpu.VMEM((16, 8, 1152), BF),
-            dma((2,)), dma((7,)), dma((7,)), dma((15,)), dma((15,)), dma((6,)), dma((6,)), dma((7,)), dma((7,)),
+            pltpu.VMEM((16, 8, 1152), BF), pltpu.VMEM((8, 16, 1152), BF), pltpu.VMEM((8, 16, 1152), BF),
+            pltpu.VMEM((2, 1024, 1024), BF), pltpu.VMEM((2, 1024, 1024), BF),
+            dma((11,)), dma((8,)), dma((7,)), dma((7,)), dma((15,)), dma((15,)), dma((12,)), dma((12,)), dma((14,)), dma((14,)),
         ],
-        compiler_params=pltpu.CompilerParams(collective_id=2, has_side_effects=True),
+        compiler_params=pltpu.CompilerParams(collective_id=2, has_side_effects=True, vmem_limit_bytes=62 * 2**20),
         name="exchange_pairs",
-    )(outgoing, text_pairs)
-
-
-WINDOW = 640
-
-
-def attend_kernel(assign, own, pairs_hbm, docs, queries, upstream, attn_out, q_grad, pair_grads, held, turned, load):
+    )(outgoing, text_pairs, weight)
+
+
+WINDOWS = (2, 3, 4, 5)
+
+
+def attend_kernel(assign, own, text_all, visual_all, docs, queries, upstream, attn_out, q_grad, pair_grads, held, turned):
     head = pl.program_id(0)
 
     @pl.when(head == 0)
     def _():
-        for block in range(16):
-            pltpu.make_async_copy(pairs_hbm.at[block], held.at[assign[block]], load.at[block]).start()
-        for block in range(16):
-            pltpu.make_async_copy(pairs_hbm.at[block], held.at[assign[block]], load.at[block]).wait()
+        row = lax.broadcasted_iota(jnp.int32, (128, 32), 0)
+        column = lax.broadcasted_iota(jnp.int32, (128, 32), 1)
+
+        def fill(source, carry):
+            begin = visual_all[source, 0:1, 1024:1025].astype(F32).astype(jnp.int32) - 1
+            spread = (row - column == begin).astype(F32).astype(BF)
+            placed = jnp.dot(spread, visual_all[source, :, 0:1024], preferred_element_type=F32)
+            inside = (row[:, 0:1] >= begin) & (row[:, 0:1] < begin + 32)
+            both = jnp.where(inside, placed, text_all[source].astype(F32)).astype(BF)
+            held[assign[2 * source]] = both[:64]
+            held[assign[2 * source + 1]] = both[64:]
+            return carry
+
+        lax.fori_loop(0, 8, fill, 0)
 
     labels = docs[...]
     starts = [jnp.sum((labels < d).astype(F32)).astype(jnp.int32) for d in (1, 2, 3)]
@@ -442,67 +533,87 @@
     score_scale = HD**-0.5
     outer = (((0,), (0,)), ((), ()))
     inner = (((1,), (1,)), ((), ()))
-    for half in range(2):
-        position = assign[own[0] * 2 + half]
-        low = jnp.maximum(position // 2 - 4, 0)
-        rows = pl.ds(half * 64, 64)
+
+    def attend(half, position, chunks):
+        window = chunks * 128
+        low = jnp.maximum(position // 2 - (chunks - 1), 0)
+        rows = pl.ds(pl.multiple_of(half * 64, 64), 64)
         query = jnp.concatenate([queries[rows, g * HD : (g + 1) * HD] for g in range(GROUP)], axis=0)
         grad = jnp.concatenate([upstream[rows, g * HD : (g + 1) * HD] for g in range(GROUP)], axis=0)
-        blocks = pl.ds(low * 2, WINDOW // 64)
-        keys = held[blocks, :, key_columns].reshape(WINDOW, HD)
-        values = held[blocks, :, value_columns].reshape(WINDOW, HD)
-        query_at = position * 64 + lax.broadcasted_iota(jnp.int32, (64, WINDOW), 0)
-        key_at = low * 128 + lax.broadcasted_iota(jnp.int32, (64, WINDOW), 1)
-        begin = jnp.zeros((64, WINDOW), jnp.int32)
+        blocks = pl.ds(low * 2, window // 64)
+        keys = held[blocks, :, key_columns].reshape(window, HD)
+        values = held[blocks, :, value_columns].reshape(window, HD)
+        query_at = position * 64 + lax.broadcasted_iota(jnp.int32, (64, window), 0)
+        key_at = low * 128 + lax.broadcasted_iota(jnp.int32, (64, window), 1)
+        begin = jnp.zeros((64, window), jnp.int32)
         for start in starts:
             begin = jnp.where(query_at >= start, start, begin)
         allowed = (key_at <= query_at) & (key_at >= begin)
-        scores = lax.dot_general(query, keys, inner, preferred_element_type=F32).reshape(GROUP, 64, WINDOW)
+        scores = lax.dot_general(query, keys, inner, preferred_element_type=F32).reshape(GROUP, 64, window)
         scores = jnp.where(allowed[None], scores * (score_scale * math.log2(math.e)), -1e30)
         weights = jnp.exp2(scores - jnp.max(scores, axis=-1, keepdims=True))
         weights = weights * (1.0 / jnp.sum(weights, axis=-1, keepdims=True))
-        weights = weights.reshape(GROUP * 64, WINDOW)
+        weights = weights.reshape(GROUP * 64, window)
         light = weights.astype(BF)
         output = jnp.dot(light, values, preferred_element_type=F32)
         weight_grad = lax.dot_general(grad, values, inner, preferred_element_type=F32)
         inner_sum = jnp.sum(weights * weight_grad, axis=-1, keepdims=True)
         score_grad = (weights * (weight_grad - inner_sum)).astype(BF)
         query_grad = jnp.dot(score_grad, keys, preferred_element_type=F32) * score_scale
-        window = pl.ds(pl.multiple_of(low * 128, 128), WINDOW)
-        turned[0, :, window] += lax.dot_general(query, score_grad, outer, preferred_element_type=F32)
-        turned[1, :, window] += lax.dot_general(grad, light, outer, preferred_element_type=F32)
+        window_at = pl.ds(pl.multiple_of(low * 128, 128), window)
+        turned[0, :, window_at] += lax.dot_general(query, score_grad, outer, preferred_element_type=F32)
+        turned[1, :, window_at] += lax.dot_general(grad, light, outer, preferred_element_type=F32)
         for g in range(GROUP):
             attn_out[rows, g * HD : (g + 1) * HD] = output[g * 64 : (g + 1) * 64].astype(BF)
             q_grad[rows, g * HD : (g + 1) * HD] = query_grad[g * 64 : (g + 1) * 64].astype(BF)
-    upright = (turned[0] * score_scale).T.reshape(16, 64, HD).astype(BF)
-    straight = turned[1].T.reshape(16, 64, HD).astype(BF)
-    held[:, :, key_columns] = upright
-    held[:, :, value_columns] = straight
+
+    def one_half(half, carry):
+        position = assign[own[0] * 2 + half]
+        begin = jnp.int32(0)
+        for start in starts:
+            begin = jnp.where(position * 64 >= start, start, begin)
+        need = position // 2 - begin // 128 + 1
+        for chunks in WINDOWS:
+            fits = need <= chunks if chunks == WINDOWS[0] else need == chunks
+
+            @pl.when(fits)
+            def _(chunks=chunks):
+                attend(half, position, chunks)
+
+        return carry
+
+    lax.fori_loop(0, 2, one_half, 0)
+    held[:, :, key_columns] = (turned[0] * score_scale).T.reshape(16, 64, HD).astype(BF)
+    held[:, :, value_columns] = turned[1].T.reshape(16, 64, HD).astype(BF)
     for block in range(16):
         pair_grads[block, :, key_columns] = held[assign[block], :, key_columns]
         pair_grads[block, :, value_columns] = held[assign[block], :, value_columns]
 
 
-def attend_call(assign, own, pairs, docs, queries, upstream):
+def attend_call(assign, own, text_all, visual_all, docs, queries, upstream):
     shape = jax.ShapeDtypeStruct
     by_head = pl.BlockSpec((128, GROUP * HD), lambda head, *_: (0, head))
+
+    def whole(*dims):
+        return pl.BlockSpec(dims, lambda head, *_: (0,) * len(dims))
+
     return pl.pallas_call(
         attend_kernel,
         out_shape=(shape((128, 4096), BF), shape((128, 4096), BF), shape((16, 64, 1024), BF)),
         grid_spec=pltpu.PrefetchScalarGridSpec(
             num_scalar_prefetch=2,
             grid=(KVH,),
-            in_specs=[ANY, pl.BlockSpec((1, 1024), lambda head, *_: (0, 0)), by_head, by_head],
-            out_specs=(by_head, by_head, pl.BlockSpec((16, 64, 1024), lambda head, *_: (0, 0, 0))),
-            scratch_shapes=[pltpu.VMEM((16, 64, 1024), BF), pltpu.VMEM((2, HD, 1024), F32), pltpu.SemaphoreType.DMA((16,))],
+            in_specs=[whole(8, 128, 1024), whole(8, 32, 1152), whole(1, 1024), by_head, by_head],
+            out_specs=(by_head, by_head, whole(16, 64, 1024)),
+            scratch_shapes=[pltpu.VMEM((16, 64, 1024), BF), pltpu.VMEM((2, HD, 1024), F32)],
         ),
-        compiler_params=pltpu.CompilerParams(vmem_limit_bytes=56 * 2**20),
+        compiler_params=pltpu.CompilerParams(vmem_limit_bytes=50 * 2**20),
         name="attend",
-    )(assign, own, pairs, docs, queries, upstream)
+    )(assign, own, text_all, visual_all, docs, queries, upstream)
 
 
 def return_kernel(
-    grads, placing, slot_of, own_grad, visual_grad,
+    grads, placing, dest, own_grad, visual_grad,
     from_partner, sums, far, plain, through, leaving, landed, turned, arrived,
     load, pair_send, pair_recv, sum_send, sum_recv, dp_send, dp_recv, ctx_send, ctx_recv,
 ):
@@ -531,36 +642,37 @@
         ring_sum.relay(chunk)
     for chunk in ORDER:
         own_grad[:, pl.ds(chunk * width, width)] = ring_sum.total(chunk).astype(BF)
-    leaving[...] = jnp.dot(placing[...], own_grad[...], preferred_element_type=F32).reshape(16, 8, 1024).astype(BF)
-    own = pltpu.make_async_copy(leaving.at[dp], landed.at[dp], load.at[0])
+    leaving[...] = jnp.dot(placing[...], own_grad[...], preferred_element_type=F32).astype(BF).reshape(8, 16, 1024)
+    own = pltpu.make_async_copy(leaving.at[ctx], landed.at[ctx], load.at[0])
     own.start()
     copies = []
-    for by in range(1, 16):
-        to = lax.rem(dp + by, 16)
-        copy = remote(leaving.at[to], landed.at[dp], dp_send.at[by - 1], dp_recv.at[by - 1], (to, ctx))
-        copy.start()
-        copies.append(copy)
-    own.wait()
-    for by in range(1, 16):
-        source = lax.rem(dp - by + 16, 16)
-        remote(landed.at[source], landed.at[source], dp_send.at[by - 1], dp_recv.at[by - 1], (source, ctx)).wait_recv()
-    row = lax.broadcasted_iota(jnp.int32, (128, 128), 0)
-    turn = (lax.broadcasted_iota(jnp.int32, (128, 128), 1) == (row % 16) * 8 + row // 16).astype(F32).astype(BF)
-    came = landed[...].astype(F32).reshape(128, 1024).astype(BF)
-    turned[...] = jnp.dot(turn, came, preferred_element_type=F32).astype(BF).reshape(8, 16, 1024)
-    own = pltpu.make_async_copy(turned.at[ctx], arrived.at[ctx], load.at[1])
-    own.start()
     for by in range(1, 8):
         to = lax.rem(ctx + by, 8)
-        copy = remote(turned.at[to], arrived.at[ctx], ctx_send.at[by - 1], ctx_recv.at[by - 1], (dp, to))
+        copy = remote(leaving.at[to], landed.at[ctx], ctx_send.at[by - 1], ctx_recv.at[by - 1], (dp, to))
         copy.start()
         copies.append(copy)
     own.wait()
     for by in range(1, 8):
         source = lax.rem(ctx - by + 8, 8)
-        remote(arrived.at[source], arrived.at[source], ctx_send.at[by - 1], ctx_recv.at[by - 1], (dp, source)).wait_recv()
-    picking = (slot_of[...] == lax.broadcasted_iota(jnp.int32, (32, 128), 1)).astype(F32).astype(BF)
-    visual_grad[...] = jnp.dot(picking, arrived[...].reshape(128, 1024), preferred_element_type=F32).astype(BF)
+        remote(landed.at[source], landed.at[source], ctx_send.at[by - 1], ctx_recv.at[by - 1], (dp, source)).wait_recv()
+    row = lax.broadcasted_iota(jnp.int32, (128, 128), 0)
+    turn = (lax.broadcasted_iota(jnp.int32, (128, 128), 1) == (row % 8) * 16 + row // 8).astype(F32).astype(BF)
+    turned[...] = jnp.dot(turn, landed[...].reshape(128, 1024), preferred_element_type=F32).reshape(16, 8, 1024).astype(BF)
+    for by in range(1, 16):
+        to = lax.rem(dp + by, 16)
+        copy = remote(turned.at[to], arrived.at[dp], dp_send.at[by - 1], dp_recv.at[by - 1], (to, ctx))
+        copy.start()
+        copies.append(copy)
+    own = pltpu.make_async_copy(turned.at[dp], arrived.at[dp], load.at[1])
+    own.start()
+    own.wait()
+    for by in range(1, 16):
+        source = lax.rem(dp - by + 16, 16)
+        remote(arrived.at[source], arrived.at[source], dp_send.at[by - 1], dp_recv.at[by - 1], (source, ctx)).wait_recv()
+    target = jnp.broadcast_to(upright(dest[...].reshape(1, 32) // 128), (32, 128))
+    picking = (target == lax.broadcasted_iota(jnp.int32, (32, 128), 1).astype(F32)).astype(F32).astype(BF)
+    came = arrived[...].astype(F32).reshape(128, 1024).astype(BF)
+    visual_grad[...] = jnp.dot(picking, came, preferred_element_type=F32).astype(BF)
     for copy in copies:
         copy.wait_send()
     for chunk in ORDER:
@@ -568,7 +680,7 @@
     ring_sum.finish()
 
 
-def return_call(grads, placing, slot_of):
+def return_call(grads, placing, dest):
     shape = jax.ShapeDtypeStruct
     dma = pltpu.SemaphoreType.DMA
     return pl.pallas_call(
@@ -579,24 +691,23 @@
         scratch_shapes=[
             pltpu.VMEM((4, 128, 1024), BF), pltpu.VMEM((4, 128, 1024), BF),
             pltpu.VMEM((4, 128, 256), BF), pltpu.VMEM((4, 128, 256), BF), pltpu.VMEM((4, 128, 256), BF),
-            pltpu.VMEM((16, 8, 1024), BF), pltpu.VMEM((16, 8, 1024), BF), pltpu.VMEM((8, 16, 1024), BF), pltpu.VMEM((8, 16, 1024), BF),
+            pltpu.VMEM((8, 16, 1024), BF), pltpu.VMEM((8, 16, 1024), BF), pltpu.VMEM((16, 8, 1024), BF), pltpu.VMEM((16, 8, 1024), BF),
             dma((2,)), dma((4,)), dma((4,)), dma((12,)), dma((12,)), dma((15,)), dma((15,)), dma((7,)), dma((7,)),
         ],
-        compiler_params=pltpu.CompilerParams(collective_id=3, has_side_effects=True),
+        compiler_params=pltpu.CompilerParams(collective_id=3, has_side_effects=True, vmem_limit_bytes=50 * 2**20),
         name="return_grads",
-    )(grads, placing, slot_of)
+    )(grads, placing, dest)
 
 
 def final_kernel(
     own_grad, visual_pair_grad, text_pairs, visual_pairs, weight, text, visual, gain, scales, marked, hidden_grad, visual_grad
 ):
-    contract = (((1,), (1,)), ((), ()))
     block = weight[...]
     gains = gain[...]
 
     def through(grad, pair, value, scale):
         mean = jnp.sum(grad.astype(F32) * pair.astype(F32), axis=-1, keepdims=True) * (1.0 / 8192.0)
-        normed_grad = lax.dot_general(grad, block, contract, preferred_element_type=F32)
+        normed_grad = jnp.dot(grad, block, preferred_element_type=F32)
         return scale * (gains * normed_grad) - value.astype(F32) * (scale * scale * mean)
 
     full = through(own_grad[...], text_pairs[...], text[...], scales[0:128, 0:1])
@@ -617,32 +728,29 @@
         grid=(8192 // tile,),
         in_specs=[
             whole(128, 1024), whole(32, 1024), whole(128, 1024), whole(32, 1024),
-            pl.BlockSpec((tile, 1024), lambda i: (i, 0)), pl.BlockSpec((128, tile), lambda i: (0, i)),
+            pl.BlockSpec((1024, tile), lambda i: (0, i)), pl.BlockSpec((128, tile), lambda i: (0, i)),
             pl.BlockSpec((32, tile), lambda i: (0, i)), pl.BlockSpec((1, tile), lambda i: (0, i)),
             whole(160, 128), whole(128, 128),
         ],
         out_specs=(pl.BlockSpec((128, tile), lambda i: (0, i)), pl.BlockSpec((32, tile), lambda i: (0, i))),
-        compiler_params=pltpu.CompilerParams(vmem_limit_bytes=48 * 2**20),
+        compiler_params=pltpu.CompilerParams(vmem_limit_bytes=52 * 2**20),
         name="through_norm",
     )(own_grad, visual_pair_grad, text_pairs, visual_pairs, weight, text, visual, gain, scales, marked)
 
 
 def local(patches, vit_gain, merge_up, merge_down, dest, text, norm_gain, kv_weight, queries, out_grad, assign, docs):
-    target = dest // 128
-    slot = (target % 8) * 16 + target // 8
-    row_of = jnp.broadcast_to((dest % 128 + 1).astype(BF)[:, None], (32, 128))
     gain = norm_gain.reshape(1, 8192)
     weight, outgoing, text_pairs, visual_pairs, visual, scales = first_call(
-        patches, vit_gain.reshape(1, 1280), merge_up, merge_down, text[0], gain, kv_weight, slot.reshape(1, 32), row_of
+        patches, vit_gain, merge_up, merge_down, text[0], gain, kv_weight, dest
     )
-    pairs, placing, marked = exchange_call(outgoing, text_pairs)
+    text_all, visual_all, placing, marked, weight_t = exchange_call(outgoing, text_pairs, weight.reshape(8192, 1024))
     own = lax.axis_index("ctx").astype(jnp.int32).reshape(1)
-    attention, query_grad, pair_grads = attend_call(assign, own, pairs.reshape(16, 64, 1024), docs, queries[0], out_grad[0])
-    own_grad, visual_pair_grad = return_call(
-        pair_grads.reshape(4, 2, 128, 1024), placing, jnp.broadcast_to(slot[:, None], (32, 128))
+    attention, query_grad, pair_grads = attend_call(
+        assign, own, text_all.reshape(8, 128, 1024), visual_all.reshape(8, 32, 1152), docs, queries[0], out_grad[0]
     )
+    own_grad, visual_pair_grad = return_call(pair_grads.reshape(4, 2, 128, 1024), placing, dest)
     hidden_grad, visual_grad = final_call(
-        own_grad, visual_pair_grad, text_pairs, visual_pairs, weight.reshape(8192, 1024), text[0], visual, gain, scales, marked
+        own_grad, visual_pair_grad, text_pairs, visual_pairs, weight_t, text[0], visual, gain, scales, marked
     )
     return attention[None], query_grad[None], hidden_grad[None], visual_grad
 

time: 172 us -> 159 us (0.924)
  Pallas kernels: 165 us -> 154 us
    pallas_call x1, Pallas kernels: 71.2 us -> 65.9 us  [first_call(): pl.pallas_call(first_kernel, out_shape=(shape((64, 2, 64, 1024), BF), sha...]
    pallas_call x1, Pallas kernels: 19.8 us -> 16.6 us  [attend_call(): pl.pallas_call(attend_kernel, out_shape=(shape((128, 4096), BF), shape((1...]
    pallas_call x1, Pallas kernels: 14.4 us -> 11.9 us  [final_call(): pl.pallas_call(final_kernel, out_shape=(shape((128, 8192), BF), shape((32...]
    unnamed x20 -> x28, local copies, waits for them, and re-layouts: 1.82 us -> 3.92 us
where the time goes in v1:
time: 159 us
  Pallas kernels  154 us (97%)
  local copies, waits for them, and re-layouts  3.92 us (2%)
    pallas_call x1, Pallas kernels, first_call(): pl.pallas_call(first_kernel, out_shape=(shape((64, 2, 64, 1024), BF), sha...  65.9 us
    pallas_call x1, Pallas kernels, return_call(): pl.pallas_call(return_kernel, out_shape=(shape((128, 1024), BF), shape((3...  31.2 us
    pallas_call x1, Pallas kernels, exchange_call(): pl.pallas_call(exchange_kernel, out_shape=(shape((4, 2, 128, 1024), BF),...  28.9 us
    pallas_call x1, Pallas kernels, attend_call(): pl.pallas_call(attend_kernel, out_shape=(shape((128, 4096), BF), shape((1...  16.6 us
    pallas_call x1, Pallas kernels, final_call(): pl.pallas_call(final_kernel, out_shape=(shape((128, 8192), BF), shape((32...  11.9 us
    unnamed x28, local copies, waits for them, and re-layouts  3.92 us

profile of v1, /device:TPU:1, one launch (start us, length us, event | category | flops | bytes accessed | tf_op | source)
XLA Modules:
  0.0 159.1 jit_solution(1761091242660621943)
XLA Ops:
  0.6 65.9 %merge_and_project.1 = (bf16[64,2,64,1024]{3,2,1,0:T(8,128)(2,1)}, bf16[16,8,1152]{2,1,0:T(8,128)(2,1)}, bf16[128,1024]{1,0:T(8,128)(2,1)}, bf16[32,1024]{1,0:T(...) custom-call(bf16[256,5120]{1,0:T(8,128)(2,1)} %patches_hbm.1, f32[1280]{0:T(1024)} %vit_gain.1, ...), custom_call_target="tpu_custom_call" | custom-call | tf_op jit(solution)/shard_map/merge_and_project/pallas_call | solution.py:342
  66.5 0.0 copy-start.2
  66.5 0.0 copy-start.11
  66.5 0.0 copy-start.13
  66.5 28.9 %exchange_pairs.1 = (bf16[4,2,128,1024]{3,2,1,0:T(8,128)(2,1)}, bf16[4,2,32,1152]{3,2,1,0:T(8,128)(2,1)}, bf16[128,128]{1,0:T(8,128)(2,1)}, f32[128,128]{1,0:T(8,128)}, bf16[1024,8192]{1,0:T(8,128)(2,1)}) custom-call(bf16[16,8,1152]{2,1,0:T(8,128)(2,1)} %get-tuple-element.22.outgoing, bf16[128,1024]{1,0:T(8,128)(2,1)} %get-tuple-element.23.text_pairs, ...), custom_call_target="tpu_custom_call" | custom-call | tf_op jit(solution)/shard_map/exchange_pairs/pallas_call | solution.py:487
  95.4 0.0 copy-start.12
  95.4 0.0 copy-done.2
  95.4 0.0 copy-done.11
  95.5 0.0 copy-done.13
  95.5 0.0 copy-start.3
  95.5 1.2 copy-done.3
  96.7 0.0 copy-start.4
  96.7 1.1 copy-done.4
  97.8 0.0 copy-start.10
  97.8 0.0 copy-start.1
  97.8 0.0 copy-start.5
  97.8 0.0 copy-start.7
  97.8 0.0 copy-start.8
  97.8 0.0 copy-start.9
  97.8 16.6 %attend.1 = (bf16[128,4096]{1,0:T(8,128)(2,1)}, bf16[128,4096]{1,0:T(8,128)(2,1)}, bf16[16,64,1024]{2,1,0:T(8,128)(2,1)}) custom-call(s32[16]{0:T(128)S(1)} %copy-done.13, s32[1]{0:T(128)} %bitcast.own, bf16[8,128,1024]{2,1,0:T(8,128)(2,1)} %bitcast.21, bf16[8,32,1152]{2,1,0:T(8,128)(2,1)S(1)} %bitcast.15, s32[1,1024]{1,0:T(1,128)S(1)} %copy-done.11, ...), custom_call_target="tpu_custom_call" | custom-call | tf_op jit(solution)/shard_map/attend/pallas_call | solution.py:600
  114.4 0.0 copy-done.12
  114.4 0.0 copy-done.10
  114.4 0.0 copy-start
  114.4 1.6 copy-done
  116.0 31.2 %return_grads.1 = (bf16[128,1024]{1,0:T(8,128)(2,1)S(1)}, bf16[32,1024]{1,0:T(8,128)(2,1)S(1)}) custom-call(bf16[4,2,128,1024]{3,2,1,0:T(8,128)(2,1)S(1)} %bitcast.12, bf16[128,128]{1,0:T(8,128)(2,1)S(1)} %copy-done.10, s32[32]{0:T(128)S(1)} %copy-done.12), custom_call_target="tpu_custom_call" | custom-call | tf_op jit(solution)/shard_map/return_grads/pallas_call | solution.py:686
  147.2 0.0 copy-done.1
  147.2 0.0 copy-done.5
  147.2 0.0 copy-done.6
  147.2 0.0 copy-done.7
  147.2 0.0 copy-done.8
  147.3 0.0 copy-done.9
  147.3 11.9 %through_norm.1 = (bf16[128,8192]{1,0:T(8,128)(2,1)}, bf16[32,8192]{1,0:T(8,128)(2,1)}) custom-call(bf16[128,1024]{1,0:T(8,128)(2,1)S(1)} %get-tuple-element.31.own_grad, bf16[32,1024]{1,0:T(8,128)(2,1)S(1)} %get-tuple-element.32.visual_pair_grad, bf16[128,1024]{1,0:T(8,128)(2,1)S(1)} %copy-done.1, bf16[32,1024]{1,0:T(8,128)(2,1)S(1)} %copy-done.8, ...), custom_call_target="tpu_custom_call" | custom-call | tf_op jit(solution)/shard_map/through_norm/pallas_call | solution.py:725
  (1 shorter events, 0.0 us)
Async XLA Ops:
  66.5 28.9 %copy-start.2 = (bf16[1,128,4096]{2,1,0:T(8,128)(2,1)S(1)}, bf16[1,128,4096]{2,1,0:T(8,128)(2,1)}, u32[]{:S(2)}) copy-start(bf16[1,128,4096]{2,1,0:T(8,128)(2,1)} %param.20) | copy-start | bytes 3145732
  66.5 28.9 %copy-start.11 = (s32[1,1024]{1,0:T(1,128)S(1)}, s32[1,1024]{1,0:T(1,128)}, u32[]{:S(2)}) copy-start(s32[1,1024]{1,0:T(1,128)} %docs.1) | copy-start | bytes 12292
  66.5 28.9 %copy-start.13 = (s32[16]{0:T(128)S(1)}, s32[16]{0:T(128)}, u32[]{:S(2)}) copy-start(s32[16]{0:T(128)} %assign.1) | copy-start | bytes 196
  95.4 18.9 %copy-start.12 = (s32[32]{0:T(128)S(1)}, s32[32]{0:T(128)}, u32[]{:S(2)}) copy-start(s32[32]{0:T(128)} %dest.3) | copy-start | bytes 388
  95.5 1.2 copy-start.3
  96.7 1.1 copy-start.4
  97.8 16.6 %copy-start.10 = (bf16[128,128]{1,0:T(8,128)(2,1)S(1)}, bf16[128,128]{1,0:T(8,128)(2,1)}, u32[]{:S(2)}) copy-start(bf16[128,128]{1,0:T(8,128)(2,1)} %get-tuple-element.30.placing) | copy-start | bytes 98308
  97.8 49.5 %copy-start.1 = (bf16[128,1024]{1,0:T(8,128)(2,1)S(1)}, bf16[128,1024]{1,0:T(8,128)(2,1)}, u32[]{:S(2)}) copy-start(bf16[128,1024]{1,0:T(8,128)(2,1)} %get-tuple-element.23.text_pairs) | copy-start | bytes 786436
  97.8 49.5 %copy-start.5 = (bf16[32,8192]{1,0:T(8,128)(2,1)S(1)}, bf16[32,8192]{1,0:T(8,128)(2,1)}, u32[]{:S(2)}) copy-start(bf16[32,8192]{1,0:T(8,128)(2,1)} %get-tuple-element.35.visual) | copy-start | bytes 1572868
  97.8 49.5 %copy-start.6 = (f32[8192]{0:T(1024)S(1)}, f32[8192]{0:T(1024)}, u32[]{:S(2)}) copy-start(f32[8192]{0:T(1024)} %param.18) | copy-start | bytes 98308
  97.8 49.5 %copy-start.7 = (f32[160,128]{1,0:T(8,128)S(1)}, f32[160,128]{1,0:T(8,128)}, u32[]{:S(2)}) copy-start(f32[160,128]{1,0:T(8,128)} %get-tuple-element.36.scales) | copy-start | bytes 245764
  97.8 49.5 %copy-start.8 = (bf16[32,1024]{1,0:T(8,128)(2,1)S(1)}, bf16[32,1024]{1,0:T(8,128)(2,1)}, u32[]{:S(2)}) copy-start(bf16[32,1024]{1,0:T(8,128)(2,1)} %get-tuple-element.33.visual_pairs) | copy-start | bytes 196612
  97.8 49.5 %copy-start.9 = (f32[128,128]{1,0:T(8,128)S(1)}, f32[128,128]{1,0:T(8,128)}, u32[]{:S(2)}) copy-start(f32[128,128]{1,0:T(8,128)} %get-tuple-element.37.marked) | copy-start | bytes 196612
  114.4 1.6 %copy-start = (bf16[16,64,1024]{2,1,0:T(8,128)(2,1)S(1)}, bf16[16,64,1024]{2,1,0:T(8,128)(2,1)}, u32[]{:S(2)}) copy-start(bf16[16,64,1024]{2,1,0:T(8,128)(2,1)} %get-tuple-element.29) | copy-start | bytes 6291460

commit v2 on v1

--- a/solution.py
+++ b/solution.py
@@ -16,6 +16,7 @@
 HD = 128
 GROUP = HEADS // KVH
 EPS = 1e-06
+VMEM_ALL = 67043328
 ANY = pl.BlockSpec(memory_space=pl.ANY)
 VM = pl.BlockSpec(memory_space=pltpu.VMEM)
 
@@ -138,14 +139,17 @@
 
 
 PARTS = ((0, 384, "yzx"), (384, 384, "xyz"), (768, 256, "zxy"))
+STEPS = (0, -1, 1, 2)
 ORDER = (0, 2, 1, 3)
 
 
 def first_kernel(
     patches_hbm, vit_gain, up_hbm, down_hbm, text_hbm, gain, kv_hbm, dest,
-    weight_out, outgoing, text_pairs, visual_pairs, visual_out, scales,
+    text_all, visual_all, placing, marked, weight_t, text_pairs, visual_pairs, visual_out, scales,
     weight, patches, up, down, text, normed, hidden, partial, from_partner, sums, far, plain, through, acc, inner,
+    outgoing, landed, turned, arrived, block_t,
     load, send, recv, forward_send, forward_recv, pair_send, pair_recv, sum_send, sum_recv, store,
+    ctx_send, ctx_recv, dp_send, dp_recv,
 ):
     at = place()
     k, y = at["k"], at["y"]
@@ -158,7 +162,8 @@
         copy.start()
         loads.append(copy)
     partner = device(shifted(at, "k", 1))
-    greet([device(shifted(at, axis, by)) for axis in "xyz" for by in (1, -1)] + [partner])
+    dp, ctx = lax.axis_index("dp"), lax.axis_index("ctx")
+    greet([(dp, lax.rem(ctx + by, 8)) for by in range(1, 8)] + [(lax.rem(dp + by, 16), ctx) for by in range(1, 16)])
     own.wait()
 
     def slab_of(axes_done, axis, first, count):
@@ -200,10 +205,14 @@
             patches[rows, columns] = (center * lax.rsqrt(spread + EPS) * vg).astype(BF)
         return carry
 
-    lax.fori_loop(0, 16, norm_rows, 0)
+    lax.fori_loop(0, 6, norm_rows, 0)
     for part in rings:
         part[0].relay()
-
+    lax.fori_loop(6, 16, norm_rows, 0)
+    for part in rings:
+        for number in (2, 3, 4, 5):
+            part[0].arrived(number)
+        part[1].start()
     loads[1].wait()
     inner[...] = jnp.zeros_like(inner)
 
@@ -213,10 +222,6 @@
         return carry
 
     lax.fori_loop(0, 5, up_step, 0)
-    for part in rings:
-        for number in (2, 3, 4, 5):
-            part[0].arrived(number)
-        part[1].start()
     value = inner[...]
     hidden[...] = (0.5 * value * (1.0 + lax.erf(value * (1.0 / math.sqrt(2.0))))).astype(BF)
     loads[2].wait()
@@ -283,29 +288,12 @@
         scale = lax.rsqrt(jnp.mean(value * value, axis=-1, keepdims=True) + EPS)
         normed[pl.ds(128 + step * 16, 16), :] = (value * scale * gain[...]).astype(BF)
         scales[pl.ds(128 + step * 16, 16), :] = jnp.broadcast_to(scale, (16, 128))
-    stores = []
-    out6 = weight_out.reshape(4, 4, 4, 2, 64, 1024)
-
-    def keep(step, numbers):
-        for number, (first, count, order) in enumerate(PARTS):
-            for each in numbers:
-                forwards[number][each].wait_recv()
-            spot = shifted(at, order[2], step)[order[2]]
-            cut = {name: (pl.ds(spot, 1) if name == order[2] else pl.ds(0, 4)) for name in "xyz"}
-            boxes = [
-                ref.at[cut["x"], cut["z"], cut["y"], :, :, pl.ds(first, count)] for ref in (weight6, out6)
-            ]
-            copy = pltpu.make_async_copy(boxes[0], boxes[1], store.at[len(stores)])
-            copy.start()
-            stores.append(copy)
-
-    keep(0, (0,))
     for number, part in enumerate(rings):
         for arrival in (4, 5):
             forward(part[2].arrived(arrival), number * 7 + 1 + arrival)
-    keep(-1, (1, 3))
-    keep(1, (2, 4))
-    keep(2, (5, 6))
+    for part in forwards:
+        for copy in part.values():
+            copy.wait_recv()
     acc[...] = jnp.zeros_like(acc)
 
     def project(step, carry):
@@ -323,89 +311,30 @@
     picking = (lax.broadcasted_iota(jnp.int32, (128, 32), 0) == entry // 128).astype(F32).astype(BF)
     outgoing[:, :, pl.ds(0, 1024)] = jnp.dot(picking, mine, preferred_element_type=F32).reshape(16, 8, 1024).astype(BF)
     outgoing[:, :, pl.ds(1024, 128)] = jnp.dot(picking, row_of, preferred_element_type=F32).reshape(16, 8, 128).astype(BF)
-    for part in rings:
-        for ring in part:
-            ring.finish()
-    for part in forwards:
-        for copy in part.values():
-            copy.wait_send()
-    for chunk in ORDER:
-        swaps[chunk].wait_send()
-    ring_sum.finish()
-    for copy in stores:
-        copy.wait()
-
-
-def first_call(patches, vit_gain, up, down, text, gain, kv, dest):
-    shape = jax.ShapeDtypeStruct
-    dma = pltpu.SemaphoreType.DMA
-    return pl.pallas_call(
-        first_kernel,
-        out_shape=(
-            shape((64, 2, 64, 1024), BF), shape((16, 8, 1152), BF), shape((128, 1024), BF), shape((32, 1024), BF),
-            shape((32, 8192), BF), shape((160, 128), F32),
-        ),
-        in_specs=[ANY, VM, ANY, ANY, ANY, VM, ANY, VM],
-        out_specs=(ANY, VM, VM, VM, VM, VM),
-        scratch_shapes=[
-            pltpu.VMEM((64, 2, 64, 1024), BF), pltpu.VMEM((256, 5120), BF), pltpu.VMEM((5120, 384), BF),
-            pltpu.VMEM((384, 8192), BF), pltpu.VMEM((128, 8192), BF), pltpu.VMEM((160, 8192), BF), pltpu.VMEM((256, 384), BF),
-            pltpu.VMEM((4, 2, 32, 8192), BF), pltpu.VMEM((4, 32, 8192), BF), pltpu.VMEM((4, 32, 8192), BF),
-            pltpu.VMEM((4, 32, 2048), BF), pltpu.VMEM((4, 32, 2048), BF), pltpu.VMEM((4, 32, 2048), BF),
-            pltpu.VMEM((160, 1024), F32), pltpu.VMEM((256, 384), F32),
-            dma((6,)), dma((54,)), dma((54,)), dma((21,)), dma((21,)), dma((4,)), dma((4,)), dma((12,)), dma((12,)), dma((12,)),
-        ],
-        compiler_params=pltpu.CompilerParams(collective_id=1, has_side_effects=True, vmem_limit_bytes=62 * 2**20),
-        name="merge_and_project",
-    )(patches, vit_gain, up, down, text, gain, kv, dest)
-
-
-def exchange_kernel(
-    outgoing, text_pairs, weight, text_all, visual_all, placing, marked, weight_t,
-    landed, turned, arrived, block, block_t,
-    load, store, ctx_send, ctx_recv, dp_send, dp_recv, send, recv, forward_send, forward_recv,
-):
-    at = place()
-    dp, ctx = lax.axis_index("dp"), lax.axis_index("ctx")
-    k, y = at["k"], at["y"]
-    own = pltpu.make_async_copy(text_pairs, text_all.at[y, k], load.at[2])
+    own = pltpu.make_async_copy(text_pairs, text_all.at[y, k], load.at[5])
     own.start()
-    fetched, stored = [], []
-
-    def fetch(chunk):
-        copy = pltpu.make_async_copy(weight.at[pl.ds(chunk * 1024, 1024)], block.at[chunk % 2], load.at[3 + chunk])
-        copy.start()
-        fetched.append(copy)
+    text_ring = Ring(at, "y", lambda coordinate, half: text_all.at[coordinate, k, pl.ds(64 * half, 64)], send, recv, 54)
+    visual_ring = Ring(at, "y", lambda coordinate, half: visual_all.at[coordinate, k, pl.ds(16 * half, 16)], send, recv, 60)
+    pair_forwards, copies, stored = [], [], []
 
     def transpose(chunk):
-        fetched[chunk].wait()
         if chunk >= 2:
             stored[chunk - 2].wait()
 
         def step(i, carry):
             lanes = pl.ds(pl.multiple_of(i * 128, 128), 128)
-            block_t[chunk % 2, :, lanes] = block[chunk % 2, lanes, :].T
+            block_t[chunk % 2, :, lanes] = weight[pl.ds(chunk * 8 + i, 1)].reshape(128, 1024).T
             return carry
 
         lax.fori_loop(0, 8, step, 0)
         copy = pltpu.make_async_copy(block_t.at[chunk % 2], weight_t.at[:, pl.ds(chunk * 1024, 1024)], store.at[chunk])
         copy.start()
         stored.append(copy)
-        if chunk + 2 < 8:
-            fetch(chunk + 2)
-
-    fetch(0)
-    fetch(1)
-    greet([(dp, lax.rem(ctx + by, 8)) for by in range(1, 8)] + [(lax.rem(dp + by, 16), ctx) for by in range(1, 16)])
-    partner = device(shifted(at, "k", 1))
-    text_ring = Ring(at, "y", lambda coordinate, half: text_all.at[coordinate, k, pl.ds(64 * half, 64)], send, recv, 0)
-    visual_ring = Ring(at, "y", lambda coordinate, half: visual_all.at[coordinate, k, pl.ds(16 * half, 16)], send, recv, 6)
-    forwards, copies = [], []
-
-    def forward(ref, number):
-        copy = remote(ref, ref, forward_send.at[number], forward_recv.at[number], partner)
-        copy.start()
-        forwards.append(copy)
+
+    def pass_on(ref, number):
+        copy = remote(ref, ref, forward_send.at[21 + number], forward_recv.at[21 + number], partner)
+        copy.start()
+        pair_forwards.append(copy)
 
     for by in range(1, 16):
         to = lax.rem(dp + by, 16)
@@ -414,14 +343,11 @@
         copies.append(copy)
     own.wait()
     text_ring.start()
-    forward(text_all.at[y, k], 0)
-    own = pltpu.make_async_copy(outgoing.at[dp], landed.at[dp], load.at[0])
+    pass_on(text_all.at[y, k], 0)
+    own = pltpu.make_async_copy(outgoing.at[dp], landed.at[dp], load.at[6])
     own.start()
     transpose(0)
     transpose(1)
-    first, second = text_ring.relay()
-    forward(first, 1)
-    forward(second, 2)
     own.wait()
     for by in range(1, 16):
         source = lax.rem(dp - by + 16, 16)
@@ -435,8 +361,11 @@
         copy = remote(turned.at[to], arrived.at[ctx], ctx_send.at[by - 1], ctx_recv.at[by - 1], (dp, to))
         copy.start()
         copies.append(copy)
-    own = pltpu.make_async_copy(turned.at[ctx], arrived.at[ctx], load.at[1])
+    own = pltpu.make_async_copy(turned.at[ctx], arrived.at[ctx], load.at[7])
     own.start()
+    first, second = text_ring.relay()
+    pass_on(first, 1)
+    pass_on(second, 2)
     transpose(2)
     transpose(3)
     own.wait()
@@ -454,24 +383,24 @@
     visual_all[y, k, :, pl.ds(0, 1024)] = packed[:32].astype(BF)
     visual_all[y, k, :, pl.ds(1024, 128)] = jnp.broadcast_to(begin, (32, 128)).astype(BF)
     visual_ring.start()
-    forward(visual_all.at[y, k], 7)
+    pass_on(visual_all.at[y, k], 7)
     places = (rows == lane + 1.0).astype(F32).astype(BF)
     placing[...] = places
     marked[...] = lax.dot_general(places, jnp.ones((128, 128), BF), contract, preferred_element_type=F32)
     transpose(4)
     for number in (2, 3, 4, 5):
-        forward(text_ring.arrived(number), number + 1)
+        pass_on(text_ring.arrived(number), number + 1)
     first, second = visual_ring.relay()
-    forward(first, 8)
-    forward(second, 9)
+    pass_on(first, 8)
+    pass_on(second, 9)
     transpose(5)
     for number in (2, 3):
-        forward(visual_ring.arrived(number), number + 8)
+        pass_on(visual_ring.arrived(number), number + 8)
     transpose(6)
     for number in (4, 5):
-        forward(visual_ring.arrived(number), number + 8)
+        pass_on(visual_ring.arrived(number), number + 8)
     transpose(7)
-    for copy in forwards:
+    for copy in pair_forwards:
         copy.wait()
     for copy in copies:
         copy.wait_send()
@@ -479,27 +408,43 @@
     visual_ring.finish()
     stored[6].wait()
     stored[7].wait()
-
-
-def exchange_call(outgoing, text_pairs, weight):
+    for part in rings:
+        for ring in part:
+            ring.finish()
+    for part in forwards:
+        for copy in part.values():
+            copy.wait_send()
+    for chunk in ORDER:
+        swaps[chunk].wait_send()
+    ring_sum.finish()
+
+
+def first_call(patches, vit_gain, up, down, text, gain, kv, dest):
     shape = jax.ShapeDtypeStruct
     dma = pltpu.SemaphoreType.DMA
     return pl.pallas_call(
-        exchange_kernel,
+        first_kernel,
         out_shape=(
             shape((4, 2, 128, 1024), BF), shape((4, 2, 32, 1152), BF), shape((128, 128), BF), shape((128, 128), F32),
-            shape((1024, 8192), BF),
+            shape((1024, 8192), BF), shape((128, 1024), BF), shape((32, 1024), BF),
+            shape((32, 8192), BF), shape((160, 128), F32),
         ),
-        in_specs=[ANY, ANY, ANY],
-        out_specs=(VM, VM, VM, VM, ANY),
+        in_specs=[ANY, VM, ANY, ANY, ANY, VM, ANY, VM],
+        out_specs=(VM, VM, VM, VM, ANY, VM, VM, VM, VM),
         scratch_shapes=[
-            pltpu.VMEM((16, 8, 1152), BF), pltpu.VMEM((8, 16, 1152), BF), pltpu.VMEM((8, 16, 1152), BF),
-            pltpu.VMEM((2, 1024, 1024), BF), pltpu.VMEM((2, 1024, 1024), BF),
-            dma((11,)), dma((8,)), dma((7,)), dma((7,)), dma((15,)), dma((15,)), dma((12,)), dma((12,)), dma((14,)), dma((14,)),
+            pltpu.VMEM((64, 2, 64, 1024), BF), pltpu.VMEM((256, 5120), BF), pltpu.VMEM((5120, 384), BF),
+            pltpu.VMEM((384, 8192), BF), pltpu.VMEM((128, 8192), BF), pltpu.VMEM((160, 8192), BF), pltpu.VMEM((256, 384), BF),
+            pltpu.VMEM((4, 2, 32, 8192), BF), pltpu.VMEM((4, 32, 8192), BF), pltpu.VMEM((4, 32, 8192), BF),
+            pltpu.VMEM((4, 32, 2048), BF), pltpu.VMEM((4, 32, 2048), BF), pltpu.VMEM((4, 32, 2048), BF),
+            pltpu.VMEM((160, 1024), F32), pltpu.VMEM((256, 384), F32),
+            pltpu.VMEM((16, 8, 1152), BF), pltpu.VMEM((16, 8, 1152), BF), pltpu.VMEM((8, 16, 1152), BF), pltpu.VMEM((8, 16, 1152), BF),
+            pltpu.VMEM((2, 1024, 1024), BF),
+            dma((8,)), dma((66,)), dma((66,)), dma((35,)), dma((35,)), dma((4,)), dma((4,)), dma((12,)), dma((12,)), dma((8,)),
+            dma((7,)), dma((7,)), dma((15,)), dma((15,)),
         ],
-        compiler_params=pltpu.CompilerParams(collective_id=2, has_side_effects=True, vmem_limit_bytes=62 * 2**20),
-        name="exchange_pairs",
-    )(outgoing, text_pairs, weight)
+        compiler_params=pltpu.CompilerParams(collective_id=1, has_side_effects=True, vmem_limit_bytes=VMEM_ALL),
+        name="merge_and_project",
+    )(patches, vit_gain, up, down, text, gain, kv, dest)
 
 
 WINDOWS = (2, 3, 4, 5)
@@ -607,19 +552,25 @@
             out_specs=(by_head, by_head, whole(16, 64, 1024)),
             scratch_shapes=[pltpu.VMEM((16, 64, 1024), BF), pltpu.VMEM((2, HD, 1024), F32)],
         ),
-        compiler_params=pltpu.CompilerParams(vmem_limit_bytes=50 * 2**20),
+        compiler_params=pltpu.CompilerParams(vmem_limit_bytes=VMEM_ALL),
         name="attend",
     )(assign, own, text_all, visual_all, docs, queries, upstream)
 
 
 def return_kernel(
-    grads, placing, dest, own_grad, visual_grad,
-    from_partner, sums, far, plain, through, leaving, landed, turned, arrived,
+    grads, placing_hbm, dest, own_grad, visual_grad,
+    kept, placing, from_partner, sums, far, plain, through, leaving, landed, turned, arrived,
     load, pair_send, pair_recv, sum_send, sum_recv, dp_send, dp_recv, ctx_send, ctx_recv,
 ):
     at = place()
     dp, ctx = lax.axis_index("dp"), lax.axis_index("ctx")
     k, y = at["k"], at["y"]
+    own = [
+        pltpu.make_async_copy(grads.at[:, k], kept, load.at[2]),
+        pltpu.make_async_copy(placing_hbm, placing, load.at[3]),
+    ]
+    for copy in own:
+        copy.start()
     greet([(dp, lax.rem(ctx + by, 8)) for by in range(1, 8)] + [(lax.rem(dp + by, 16), ctx) for by in range(1, 16)])
     partner = device(shifted(at, "k", 1))
     width = 256
@@ -631,11 +582,13 @@
         )
         swaps[chunk].start()
     ring_sum = RingSum(at, sums, far, plain, through, 4, sum_send, sum_recv)
+    for copy in own:
+        copy.wait()
     for chunk in ORDER:
         swaps[chunk].wait_recv()
         columns = pl.ds(chunk * width, width)
         for block in range(4):
-            mine = grads[block, pl.ds(k, 1), :, columns].reshape(128, width)
+            mine = kept[block, :, columns]
             sums[block, :, columns] = (mine.astype(F32) + from_partner[block, :, columns].astype(F32)).astype(BF)
         ring_sum.start(chunk)
     for chunk in ORDER:
@@ -686,15 +639,16 @@
     return pl.pallas_call(
         return_kernel,
         out_shape=(shape((128, 1024), BF), shape((32, 1024), BF)),
-        in_specs=[VM, VM, VM],
+        in_specs=[ANY, ANY, VM],
         out_specs=(VM, VM),
         scratch_shapes=[
+            pltpu.VMEM((4, 128, 1024), BF), pltpu.VMEM((128, 128), BF),
             pltpu.VMEM((4, 128, 1024), BF), pltpu.VMEM((4, 128, 1024), BF),
             pltpu.VMEM((4, 128, 256), BF), pltpu.VMEM((4, 128, 256), BF), pltpu.VMEM((4, 128, 256), BF),
             pltpu.VMEM((8, 16, 1024), BF), pltpu.VMEM((8, 16, 1024), BF), pltpu.VMEM((16, 8, 1024), BF), pltpu.VMEM((16, 8, 1024), BF),
-            dma((2,)), dma((4,)), dma((4,)), dma((12,)), dma((12,)), dma((15,)), dma((15,)), dma((7,)), dma((7,)),
+            dma((4,)), dma((4,)), dma((4,)), dma((12,)), dma((12,)), dma((15,)), dma((15,)), dma((7,)), dma((7,)),
         ],
-        compiler_params=pltpu.CompilerParams(collective_id=3, has_side_effects=True, vmem_limit_bytes=50 * 2**20),
+        compiler_params=pltpu.CompilerParams(collective_id=3, has_side_effects=True, vmem_limit_bytes=VMEM_ALL),
         name="return_grads",
     )(grads, placing, dest)
 
@@ -733,17 +687,16 @@
             whole(160, 128), whole(128, 128),
         ],
         out_specs=(pl.BlockSpec((128, tile), lambda i: (0, i)), pl.BlockSpec((32, tile), lambda i: (0, i))),
-        compiler_params=pltpu.CompilerParams(vmem_limit_bytes=52 * 2**20),
+        compiler_params=pltpu.CompilerParams(vmem_limit_bytes=VMEM_ALL),
         name="through_norm",
     )(own_grad, visual_pair_grad, text_pairs, visual_pairs, weight, text, visual, gain, scales, marked)
 
 
 def local(patches, vit_gain, merge_up, merge_down, dest, text, norm_gain, kv_weight, queries, out_grad, assign, docs):
     gain = norm_gain.reshape(1, 8192)
-    weight, outgoing, text_pairs, visual_pairs, visual, scales = first_call(
+    text_all, visual_all, placing, marked, weight_t, text_pairs, visual_pairs, visual, scales = first_call(
         patches, vit_gain, merge_up, merge_down, text[0], gain, kv_weight, dest
     )
-    text_all, visual_all, placing, marked, weight_t = exchange_call(outgoing, text_pairs, weight.reshape(8192, 1024))
     own = lax.axis_index("ctx").astype(jnp.int32).reshape(1)
     attention, query_grad, pair_grads = attend_call(
         assign, own, text_all.reshape(8, 128, 1024), visual_all.reshape(8, 32, 1152), docs, queries[0], out_grad[0]

time: 159 us -> 152 us (0.956)
  local copies, waits for them, and re-layouts: 3.92 us -> 0 us
  Pallas kernels: 154 us -> 151 us
    pallas_call x2 -> x1, Pallas kernels: 94.7 us -> 88.7 us  [first_call(): pl.pallas_call(first_kernel, out_shape=(shape((4, 2, 128, 1024), BF), sha...]
    unnamed x28 -> x0, local copies, waits for them, and re-layouts: 3.92 us -> none
    pallas_call x1, Pallas kernels: 31.2 us -> 33.8 us  [return_call(): pl.pallas_call(return_kernel, out_shape=(shape((128, 1024), BF), shape((3...]
where the time goes in v2:
time: 152 us; the launch traced here: 151 us
  Pallas kernels  151 us (99%)
    pallas_call x1, Pallas kernels, first_call(): pl.pallas_call(first_kernel, out_shape=(shape((4, 2, 128, 1024), BF), sha...  88.7 us
    pallas_call x1, Pallas kernels, return_call(): pl.pallas_call(return_kernel, out_shape=(shape((128, 1024), BF), shape((3...  33.8 us
    pallas_call x1, Pallas kernels, attend_call(): pl.pallas_call(attend_kernel, out_shape=(shape((128, 4096), BF), shape((1...  15.6 us
    pallas_call x1, Pallas kernels, final_call(): pl.pallas_call(final_kernel, out_shape=(shape((128, 8192), BF), shape((32...  12.5 us

profile of v2, /device:TPU:1, one launch (start us, length us, event | category | flops | bytes accessed | tf_op | source)
XLA Modules:
  0.0 151.2 jit_solution(14352415650754537926)
XLA Ops:
  0.6 88.7 %merge_and_project.1 = (bf16[4,2,128,1024]{3,2,1,0:T(8,128)(2,1)}, bf16[4,2,32,1152]{3,2,1,0:T(8,128)(2,1)}, bf16[128,128]{1,0:T(8,128)(2,1)}, f32[128,128]{1,0:...) custom-call(bf16[256,5120]{1,0:T(8,128)(2,1)} %patches_hbm.1, ...), custom_call_target="tpu_custom_call" | custom-call | tf_op jit(solution)/shard_map/merge_and_project/pallas_call | solution.py:425
  89.3 15.6 %attend.1 = (bf16[128,4096]{1,0:T(8,128)(2,1)}, bf16[128,4096]{1,0:T(8,128)(2,1)}, bf16[16,64,1024]{2,1,0:T(8,128)(2,1)}) custom-call(s32[16]{0:T(128)} %assign.1, s32[1]{0:T(128)} %bitcast.own, bf16[8,128,1024]{2,1,0:T(8,128)(2,1)} %bitcast.14, bf16[8,32,1152]{2,1,0:T(8,128)(2,1)} %bitcast.17, s32[1,1024]{1,0:T(1,128)} %docs.1, bf16[128,4096]{1,0:T(8,128)(2,1)} %bitcast.15, ...), custom_call_target="tpu_custom_call" | custom-call | tf_op jit(solution)/shard_map/attend/pallas_call | solution.py:545
  104.9 33.8 %return_grads.1 = (bf16[128,1024]{1,0:T(8,128)(2,1)}, bf16[32,1024]{1,0:T(8,128)(2,1)}) custom-call(bf16[4,2,128,1024]{3,2,1,0:T(8,128)(2,1)} %bitcast.13, bf16[128,128]{1,0:T(8,128)(2,1)} %get-tuple-element.25.placing_hbm, s32[32]{0:T(128)} %dest.3), custom_call_target="tpu_custom_call" | custom-call | tf_op jit(solution)/shard_map/return_grads/pallas_call | solution.py:639
  138.7 12.5 %through_norm.1 = (bf16[128,8192]{1,0:T(8,128)(2,1)}, bf16[32,8192]{1,0:T(8,128)(2,1)}) custom-call(bf16[128,1024]{1,0:T(8,128)(2,1)} %get-tuple-element.26.own_grad, bf16[32,1024]{1,0:T(8,128)(2,1)} %get-tuple-element.27.visual_pair_grad, bf16[128,1024]{1,0:T(8,128)(2,1)} %get-tuple-element.28.text_pairs, bf16[32,1024]{1,0:T(8,128)(2,1)} %get-tuple-element.29.visual_pairs, ...), custom_call_target="tpu_custom_call" | custom-call | tf_op jit(solution)/shard_map/through_norm/pallas_call | solution.py:679

commit v3 on v2

--- a/solution.py
+++ b/solution.py
@@ -654,24 +654,29 @@
 
 
 def final_kernel(
-    own_grad, visual_pair_grad, text_pairs, visual_pairs, weight, text, visual, gain, scales, marked, hidden_grad, visual_grad
+    own_grad, visual_pair_grad, text_pairs, visual_pairs, weight, text, visual, gain, scales, marked, hidden_grad, visual_grad, means
 ):
+    @pl.when(pl.program_id(0) == 0)
+    def _():
+        for rows, grad, pair in ((pl.ds(0, 128), own_grad, text_pairs), (pl.ds(128, 32), visual_pair_grad, visual_pairs)):
+            mean = jnp.sum(grad[...].astype(F32) * pair[...].astype(F32), axis=-1, keepdims=True) * (1.0 / 8192.0)
+            means[rows, :] = jnp.broadcast_to(mean, (rows.size, 128))
+
     block = weight[...]
     gains = gain[...]
 
-    def through(grad, pair, value, scale):
-        mean = jnp.sum(grad.astype(F32) * pair.astype(F32), axis=-1, keepdims=True) * (1.0 / 8192.0)
+    def through(grad, mean, value, scale):
         normed_grad = jnp.dot(grad, block, preferred_element_type=F32)
         return scale * (gains * normed_grad) - value.astype(F32) * (scale * scale * mean)
 
-    full = through(own_grad[...], text_pairs[...], text[...], scales[0:128, 0:1])
+    full = through(own_grad[...], means[0:128, 0:1], text[...], scales[0:128, 0:1])
     hidden_grad[...] = jnp.where(marked[:, 0:1] > 0.5, 0.0, full).astype(BF)
-    visual_grad[...] = through(visual_pair_grad[...], visual_pairs[...], visual[...], scales[128:160, 0:1]).astype(BF)
+    visual_grad[...] = through(visual_pair_grad[...], means[128:160, 0:1], visual[...], scales[128:160, 0:1]).astype(BF)
 
 
 def final_call(own_grad, visual_pair_grad, text_pairs, visual_pairs, weight, text, visual, gain, scales, marked):
     shape = jax.ShapeDtypeStruct
-    tile = 1024
+    tile = 2048
 
     def whole(*dims):
         return pl.BlockSpec(dims, lambda i: (0,) * len(dims))
@@ -687,6 +692,7 @@
             whole(160, 128), whole(128, 128),
         ],
         out_specs=(pl.BlockSpec((128, tile), lambda i: (0, i)), pl.BlockSpec((32, tile), lambda i: (0, i))),
+        scratch_shapes=[pltpu.VMEM((160, 128), F32)],
         compiler_params=pltpu.CompilerParams(vmem_limit_bytes=VMEM_ALL),
         name="through_norm",
     )(own_grad, visual_pair_grad, text_pairs, visual_pairs, weight, text, visual, gain, scales, marked)

time: 152 us -> 151 us (level)
    pallas_call x1, Pallas kernels: 12.5 us -> 10.9 us  [final_call(): pl.pallas_call(final_kernel, out_shape=(shape((128, 8192), BF), shape((32...]
where the time goes in v3:
time: 151 us
  Pallas kernels  150 us (99%)
    pallas_call x1, Pallas kernels, first_call(): pl.pallas_call(first_kernel, out_shape=(shape((4, 2, 128, 1024), BF), sha...  88.7 us
    pallas_call x1, Pallas kernels, return_call(): pl.pallas_call(return_kernel, out_shape=(shape((128, 1024), BF), shape((3...  35.1 us
    pallas_call x1, Pallas kernels, attend_call(): pl.pallas_call(attend_kernel, out_shape=(shape((128, 4096), BF), shape((1...  15.6 us
    pallas_call x1, Pallas kernels, final_call(): pl.pallas_call(final_kernel, out_shape=(shape((128, 8192), BF), shape((32...  10.9 us

profile of v3, /device:TPU:1, one launch (start us, length us, event | category | flops | bytes accessed | tf_op | source)
XLA Modules:
  0.0 150.9 jit_solution(14783063175865951661)
XLA Ops:
  0.6 88.7 %merge_and_project.1 = (bf16[4,2,128,1024]{3,2,1,0:T(8,128)(2,1)}, bf16[4,2,32,1152]{3,2,1,0:T(8,128)(2,1)}, bf16[128,128]{1,0:T(8,128)(2,1)}, f32[128,128]{1,0:...) custom-call(bf16[256,5120]{1,0:T(8,128)(2,1)} %patches_hbm.1, ...), custom_call_target="tpu_custom_call" | custom-call | tf_op jit(solution)/shard_map/merge_and_project/pallas_call | solution.py:425
  89.3 15.6 %attend.1 = (bf16[128,4096]{1,0:T(8,128)(2,1)}, bf16[128,4096]{1,0:T(8,128)(2,1)}, bf16[16,64,1024]{2,1,0:T(8,128)(2,1)}) custom-call(s32[16]{0:T(128)} %assign.1, s32[1]{0:T(128)} %bitcast.own, bf16[8,128,1024]{2,1,0:T(8,128)(2,1)} %bitcast.14, bf16[8,32,1152]{2,1,0:T(8,128)(2,1)} %bitcast.17, s32[1,1024]{1,0:T(1,128)} %docs.1, bf16[128,4096]{1,0:T(8,128)(2,1)} %bitcast.15, ...), custom_call_target="tpu_custom_call" | custom-call | tf_op jit(solution)/shard_map/attend/pallas_call | solution.py:545
  104.9 35.1 %return_grads.1 = (bf16[128,1024]{1,0:T(8,128)(2,1)}, bf16[32,1024]{1,0:T(8,128)(2,1)}) custom-call(bf16[4,2,128,1024]{3,2,1,0:T(8,128)(2,1)} %bitcast.13, bf16[128,128]{1,0:T(8,128)(2,1)} %get-tuple-element.25.placing_hbm, s32[32]{0:T(128)} %dest.3), custom_call_target="tpu_custom_call" | custom-call | tf_op jit(solution)/shard_map/return_grads/pallas_call | solution.py:639
  140.0 10.9 %through_norm.1 = (bf16[128,8192]{1,0:T(8,128)(2,1)}, bf16[32,8192]{1,0:T(8,128)(2,1)}) custom-call(bf16[128,1024]{1,0:T(8,128)(2,1)} %get-tuple-element.26.own_grad, bf16[32,1024]{1,0:T(8,128)(2,1)} %get-tuple-element.27.visual_pair_grad, bf16[128,1024]{1,0:T(8,128)(2,1)} %get-tuple-element.28.text_pairs, bf16[32,1024]{1,0:T(8,128)(2,1)} %get-tuple-element.29.visual_pairs, ...), custom_call_target="tpu_custom_call" | custom-call | tf_op jit(solution)/shard_map/through_norm/pallas_call | solution.py:684
